TPU v7x, 512 devices: a whole 4x4x16 slice. The times are simulated.
512 devices in a mesh: level: 16 (over z_lo, core), space: 32 (over x, z_hi, y).
Axes of the slice: x: 4, y: 4, z: 16 (z_hi: 2, z_lo: 8; z = z_hi * 8 + z_lo), core: 2. Of those that a mesh axis runs over, the one named last changes fastest.
Arguments:
- fc_long: bfloat16 [704, 16, 8, 3, 1440], P('space', 'level'), may hold values from -6 to 6
- fc_short: bfloat16 [704, 16, 8, 3, 1440], P('space', 'level'), may hold values from -6 to 6
Outputs:
- cross: float32 [2, 3, 16, 16, 448, 384], P(None, None, 'level', None, 'space')
All inputs are finite; a program needn't handle non-finite values.
Results may differ from a plain program's by a relative error of at most 0.0077.
Values may be sent and summed in bfloat16 or wider, within the bound.
No kernel may reach another device: no remote copies, remote signals or barrier semaphores. Data moves between devices by JAX's collectives and lax.ppermute only.
A program may use at most 64 MiB of HBM per device.

v0:
```python
import math

import jax
import jax.numpy as jnp
from jax import lax
from jax.sharding import PartitionSpec as P

LAT = 704
MK = 448
NL = 384


def from_behind(block, axis, distance):
    devices = range(lax.axis_size(axis))
    route = [((i - distance) % len(devices), i) for i in devices]
    return lax.ppermute(block, axis, route)


def zonal_table(lon_size, wave_total, space_size):
    wave_local = wave_total // space_size
    lon_index = jnp.arange(lon_size, dtype=jnp.int32)[:, None, None]
    wave_index = (
        jnp.arange(space_size, dtype=jnp.int32)[:, None] * wave_local
        + jnp.arange(wave_local, dtype=jnp.int32)[None, :]
    )[None]
    phase_int = lon_index * wave_index % lon_size
    angle_rad = 2.0 * math.pi / lon_size * phase_int.astype(jnp.float32)
    table = jnp.stack([jnp.cos(angle_rad), -jnp.sin(angle_rad)], axis=2) / math.sqrt(lon_size)
    return table.astype(jnp.bfloat16)


def merid_table(lat_size, wave_total):
    lat_index = jnp.arange(lat_size, dtype=jnp.int32)[:, None]
    wave_index = jnp.arange(wave_total, dtype=jnp.int32)[None, :] - wave_total // 2
    phase_int = lat_index * wave_index % lat_size
    angle_rad = 2.0 * math.pi / lat_size * phase_int.astype(jnp.float32)
    table = jnp.stack([jnp.cos(angle_rad), jnp.sin(angle_rad)], axis=1) / math.sqrt(lat_size)
    return table.astype(jnp.bfloat16)


def cross_pair(own_spec, other_spec):
    own_spec = own_spec.astype(jnp.float32)
    other_spec = other_spec.astype(jnp.float32)
    pattern = "savkl,sbvkl->vabkl"
    highest = lax.Precision.HIGHEST
    co_spec = jnp.einsum(pattern, own_spec[0], other_spec[0], precision=highest) + jnp.einsum(
        pattern, own_spec[1], other_spec[1], precision=highest
    )
    quad_spec = jnp.einsum(pattern, own_spec[1], other_spec[0], precision=highest) - jnp.einsum(
        pattern, own_spec[0], other_spec[1], precision=highest
    )
    return jnp.stack([co_spec, quad_spec]) / own_spec.shape[1]


def mirror(pair_result):
    return jnp.stack([jnp.swapaxes(pair_result[0], 1, 2), -jnp.swapaxes(pair_result[1], 1, 2)])


def on_device(fc_long, fc_short):
    lat_local, lev_local, sample_count, var_count, lon_size = fc_long.shape
    space_size = lax.axis_size("space")
    wave_local = MK // space_size
    diff_field = (fc_long.astype(jnp.float32) - fc_short.astype(jnp.float32)).astype(jnp.bfloat16)
    zonal_tab = zonal_table(lon_size, MK, space_size)
    merid_tab = merid_table(LAT, NL)
    zonal_coeff = jnp.einsum(
        "yasvx,xpuk->ypsavuk", diff_field, zonal_tab, preferred_element_type=jnp.float32
    ).astype(jnp.bfloat16)
    zonal_coeff = zonal_coeff.reshape(
        lat_local, space_size, sample_count, lev_local * var_count * 2 * wave_local
    )
    columns = lax.all_to_all(zonal_coeff, "space", split_axis=1, concat_axis=0, tiled=True)
    total_lat, unused_one, item_count, row_width = columns.shape
    columns = columns.reshape(total_lat, item_count, lev_local, var_count, 2, wave_local)
    products = jnp.einsum(
        "ysavuk,ytl->savuktl", columns, merid_tab, preferred_element_type=jnp.float32
    )
    real_part = products[:, :, :, 0, :, 0, :] + products[:, :, :, 1, :, 1, :]
    imag_part = products[:, :, :, 1, :, 0, :] - products[:, :, :, 0, :, 1, :]
    spectra = jnp.stack([real_part, imag_part]).astype(jnp.bfloat16)
    level_size = lax.axis_size("level")
    half_loop = level_size // 2
    own_index = lax.axis_index("level")
    blocks = [None] * level_size
    blocks[0] = cross_pair(spectra, spectra)
    partner = spectra
    for offset in range(1, half_loop + 1):
        partner = from_behind(spectra, "level", offset)
        lower_pair = cross_pair(spectra, partner)
        blocks[level_size - offset] = lower_pair
        if offset < level_size - offset:
            blocks[offset] = from_behind(mirror(lower_pair), "level", -offset)
    assembled = jnp.stack(blocks, axis=3)
    assembled = jnp.roll(assembled, own_index * 1, axis=3)
    return assembled.reshape(2, var_count, lev_local, level_size * lev_local, wave_local, NL)


def solution(mesh):
    placed = (P("space", "level", None, None, None), P("space", "level", None, None, None))
    return jax.shard_map(
        on_device,
        mesh=mesh,
        in_specs=placed,
        out_specs=P(None, None, "level", None, "space", None),
        check_vma=False,
    )
```

profile of v0, /device:TPU:1, one launch (start us, length us, event | category | flops | bytes accessed | tf_op | source)
XLA Modules:
  0.0 408.2 jit_solution(14462521958171438487)
XLA Ops:
  0.0 11.7 %fusion.9 = (f32[1440,32,1,14]{0,1,3,2:T(8,128)S(1)}, f32[1440,32,1,14]{0,1,3,2:T(8,128)S(1)}) fusion(s32[32,14]{0,1:T(8,128)S(1)} %iota_add_fusion), kind=kLoop, calls=%fused_computation.49 | loop fusion | flops 6451200 | bytes 5162752 | tf_op jit(solution)/shard_map/cos | solution.py:28
  12.2 7.4 %convert_bitcast_fusion = bf16[22,32,8,1,3,2,14]{1,0,4,2,6,5,3:T(8,128)(2,1)S(1)} fusion(f32[1440,32,1,14]{0,1,3,2:T(8,128)S(1)} %get-tuple-element.261, f32[1440,32,1,14]{0,1,3,2:T(8,128)S(1)} %get-tuple-element.260, bf16[22,8,3,1440,1,1]{3,1,2,0,5,4:T(8,128)(2,1)S(1)} %fusion.15), kind=kOutput, calls=%fused_computation.2 | convolution fusion | flops 1366837248 | bytes 7627776 | tf_op jit(solution)/shard_map/yasvx,xpuk->ypsavuk/dot_general | solution.py:66
  19.6 2.5 copy.173
  22.0 5.4 %copy.174 = bf16[22,32,8,84]{3,2,0,1:T(8,128)(2,1)} copy(bf16[22,32,8,84]{1,2,3,0:T(8,128)(2,1)} %bitcast.364) | data formatting | bytes 1892352 | tf_op jit(solution)/shard_map/reshape | solution.py:69
  27.4 21.1 %all-to-all-start = ((bf16[22,32,8,84]{3,2,0,1:T(8,128)(2,1)}), bf16[22,32,8,84]{3,2,0,1:T(8,128)(2,1)S(1)}, u32[]{:S(2)}, u32[]{:S(2)}) async-start(bf16[22,32,8,84]{3,2,0,1:T(8,128)(2,1)} %copy.174), calls=%async_computation | async-start | bytes 2883584 | tf_op jit(solution)/shard_map/all_to_all | solution.py:72
  48.5 5.7 %fusion.25 = (f32[704,1,384]{2,0,1:T(8,128)}, f32[704,1,384]{2,0,1:T(8,128)}) fusion(s32[384]{0:T(512)S(1)} %iota_add_fusion.1), kind=kLoop, calls=%fused_computation.67 | loop fusion | flops 2433024 | bytes 2164224 | tf_op jit(solution)/shard_map/cos | solution.py:37
  54.3 32.8 %all-to-all-done = bf16[22,32,8,84]{3,2,0,1:T(8,128)(2,1)S(1)} async-done(((bf16[22,32,8,84]{3,2,0,1:T(8,128)(2,1)}), bf16[22,32,8,84]{3,2,0,1:T(8,128)(2,1)S(1)}, u32[]{:S(2)}, u32[]{:S(2)}) %all-to-all-start) | async-done | bytes 946208 | tf_op jit(solution)/shard_map/all_to_all | solution.py:72
  87.0 4.8 %copy.439 = bf16[32,22,1,8,84]{1,0,4,3,2:T(8,128)(2,1)} copy(bf16[32,22,1,8,84]{4,3,1,0,2:T(8,128)(2,1)S(1)} %bitcast.365) | data formatting | bytes 1892352 | tf_op jit(solution)/shard_map/reshape.6
  91.9 11.0 %reshape.1146 = bf16[704,8,3,2,14,1]{0,4,3,2,1,5:T(8,128)(2,1)S(1)} reshape(bf16[32,22,1,8,84]{1,0,4,3,2:T(8,128)(2,1)} %copy.439) | data formatting | bytes 1892352 | tf_op jit(solution)/shard_map/reshape.6
  102.8 2.6 convolution_bitcast_fusion
  106.7 40.7 %collective-permute-start = (bf16[2,8,1,3,14,384]{5,1,4,3,2,0:T(8,128)(2,1)}, bf16[2,8,1,3,14,384]{5,1,4,3,2,0:T(8,128)(2,1)}, u32[]{:S(2)}, u32[]{:S(2)}) collective-permute-start(bf16[2,8,1,3,14,384]{5,1,4,3,2,0:T(8,128)(2,1)} %copy.179), channel_id=1, source_target_pairs={{480,0},{0,32},{32,64},{64,96},{96,128},{128,160},{160,192},{192,2... | collective-permute-start | bytes 1548296 | tf_op jit(solution)/shard_map/ppermute | solution.py:16
  147.4 1.9 collective-permute-start.2
  149.3 1.9 collective-permute-start.4
  153.2 5.3 %collective-permute-start.8 = (bf16[2,8,1,3,14,384]{5,1,4,3,2,0:T(8,128)(2,1)}, bf16[2,8,1,3,14,384]{5,1,4,3,2,0:T(8,128)(2,1)S(1)}, u32[]{:S(2)}, u32[]{:S(2)}) collective-permute-start(bf16[2,8,1,3,14,384]{5,1,4,3,2,0:T(8,128)(2,1)} %copy.179), channel_id=1, source_target_pairs={{352,0},{384,32},{416,64},{448,96},{480,128},{0,160},{32,192},{64,... | collective-permute-start | bytes 1548296 | tf_op jit(solution)/shard_map/ppermute | solution.py:16
  158.4 7.5 %collective-permute-start.10 = (bf16[2,8,1,3,14,384]{5,1,4,3,2,0:T(8,128)(2,1)}, bf16[2,8,1,3,14,384]{5,1,4,3,2,0:T(8,128)(2,1)S(1)}, u32[]{:S(2)}, u32[]{:S(2)}) collective-permute-start(bf16[2,8,1,3,14,384]{5,1,4,3,2,0:T(8,128)(2,1)} %copy.179), channel_id=1, source_target_pairs={{320,0},{352,32},{384,64},{416,96},{448,128},{480,160},{0,192},{32... | collective-permute-start | bytes 1548296 | tf_op jit(solution)/shard_map/ppermute | solution.py:16
  167.8 3.4 collective-permute-start.12
  171.2 7.7 %collective-permute-done.4 = bf16[2,8,1,3,14,384]{5,1,4,3,2,0:T(8,128)(2,1)S(1)} collective-permute-done((bf16[2,8,1,3,14,384]{5,1,4,3,2,0:T(8,128)(2,1)}, bf16[2,8,1,3,14,384]{5,1,4,3,2,0:T(8,128)(2,1)S(1)}, u32[]{:S(2)}, u32[]{:S(2)}) %collective-permute-start.4) | collective-permute-done | bytes 516128 | tf_op jit(solution)/shard_map/ppermute | solution.py:16
  178.9 2.1 collective-permute-start.14
  181.1 71.5 %collective-permute-done.6 = bf16[2,8,1,3,14,384]{5,1,4,3,2,0:T(8,128)(2,1)S(1)} collective-permute-done((bf16[2,8,1,3,14,384]{5,1,4,3,2,0:T(8,128)(2,1)}, bf16[2,8,1,3,14,384]{5,1,4,3,2,0:T(8,128)(2,1)S(1)}, u32[]{:S(2)}, u32[]{:S(2)}) %collective-permute-start.6) | collective-permute-done | bytes 516128 | tf_op jit(solution)/shard_map/ppermute | solution.py:16
  252.9 60.5 %collective-permute-done.10 = bf16[2,8,1,3,14,384]{5,1,4,3,2,0:T(8,128)(2,1)S(1)} collective-permute-done((bf16[2,8,1,3,14,384]{5,1,4,3,2,0:T(8,128)(2,1)}, bf16[2,8,1,3,14,384]{5,1,4,3,2,0:T(8,128)(2,1)S(1)}, u32[]{:S(2)}, u32[]{:S(2)}) %collective-permute-start.10) | collective-permute-done | bytes 516128 | tf_op jit(solution)/shard_map/ppermute | solution.py:16
  313.6 40.8 %collective-permute-done.14 = bf16[2,8,1,3,14,384]{5,1,4,3,2,0:T(8,128)(2,1)S(1)} collective-permute-done((bf16[2,8,1,3,14,384]{5,1,4,3,2,0:T(8,128)(2,1)}, bf16[2,8,1,3,14,384]{5,1,4,3,2,0:T(8,128)(2,1)S(1)}, u32[]{:S(2)}, u32[]{:S(2)}) %collective-permute-start.14) | collective-permute-done | bytes 516128 | tf_op jit(solution)/shard_map/ppermute | solution.py:16
  354.5 3.4 fusion.33
  358.1 1.9 collective-permute-start.13
  360.2 1.9 collective-permute-start.11
  362.2 4.6 %collective-permute-start.9 = (f32[2,3,1,1,14,384]{5,4,1,3,2,0:T(8,128)S(1)}, f32[2,3,1,1,14,384]{5,4,1,3,2,0:T(8,128)S(1)}, u32[]{:S(2)}, u32[]{:S(2)}) collective-permute-start(f32[2,3,1,1,14,384]{5,4,1,3,2,0:T(8,128)S(1)} %pad_maximum_fusion.5), channel_id=1, source_target_pairs={{160,0},{192,32},{224,64},{256,96},{288,128},{320,160},{352,192},{... | collective-permute-start | bytes 387080 | tf_op jit(solution)/shard_map/ppermute | solution.py:16
  366.8 7.0 %collective-permute-start.7 = (f32[2,3,1,1,14,384]{5,4,1,3,2,0:T(8,128)S(1)}, f32[2,3,1,1,14,384]{5,4,1,3,2,0:T(8,128)S(1)}, u32[]{:S(2)}, u32[]{:S(2)}) collective-permute-start(f32[2,3,1,1,14,384]{5,4,1,3,2,0:T(8,128)S(1)} %pad_maximum_fusion.4), channel_id=1, source_target_pairs={{128,0},{160,32},{192,64},{224,96},{256,128},{288,160},{320,192},{... | collective-permute-start | bytes 387080 | tf_op jit(solution)/shard_map/ppermute | solution.py:16
  374.1 2.3 collective-permute-start.1
  377.0 4.2 %collective-permute-done.1 = f32[2,3,1,1,14,384]{5,4,1,3,2,0:T(8,128)S(1)} collective-permute-done((f32[2,3,1,1,14,384]{5,4,1,3,2,0:T(8,128)S(1)}, f32[2,3,1,1,14,384]{5,4,1,3,2,0:T(8,128)S(1)}, u32[]{:S(2)}, u32[]{:S(2)}) %collective-permute-start.1) | collective-permute-done | bytes 129056 | tf_op jit(solution)/shard_map/ppermute | solution.py:16
  381.2 9.1 %collective-permute-start.3 = (f32[2,3,1,1,14,384]{5,4,1,3,2,0:T(8,128)S(1)}, f32[2,3,1,1,14,384]{5,4,1,3,2,0:T(8,128)S(1)}, u32[]{:S(2)}, u32[]{:S(2)}) collective-permute-start(f32[2,3,1,1,14,384]{5,4,1,3,2,0:T(8,128)S(1)} %pad_maximum_fusion.2), channel_id=1, source_target_pairs={{64,0},{96,32},{128,64},{160,96},{192,128},{224,160},{256,192},{28... | collective-permute-start | bytes 387080 | tf_op jit(solution)/shard_map/ppermute | solution.py:16
  390.4 2.0 collective-permute-done.3
  392.4 3.7 collective-permute-start.5
  396.2 6.8 %collective-permute-done.5 = f32[2,3,1,1,14,384]{5,4,1,3,2,0:T(8,128)S(1)} collective-permute-done((f32[2,3,1,1,14,384]{5,4,1,3,2,0:T(8,128)S(1)}, f32[2,3,1,1,14,384]{5,4,1,3,2,0:T(8,128)S(1)}, u32[]{:S(2)}, u32[]{:S(2)}) %collective-permute-start.5) | collective-permute-done | bytes 129056 | tf_op jit(solution)/shard_map/ppermute | solution.py:16
  (108 shorter events, 12.4 us)
Async XLA Ops:
  0.0 11.8 %copy-start.1 = (bf16[22,1,8,3,1440]{4,2,3,1,0:T(8,128)(2,1)S(1)}, bf16[22,1,8,3,1440]{4,2,3,1,0:T(8,128)(2,1)}, u32[]{:S(2)}) copy-start(bf16[22,1,8,3,1440]{4,2,3,1,0:T(8,128)(2,1)} %param.2) | copy-start | bytes 4561924
  0.0 11.8 %copy-start = (bf16[22,1,8,3,1440]{4,2,3,1,0:T(8,128)(2,1)S(1)}, bf16[22,1,8,3,1440]{4,2,3,1,0:T(8,128)(2,1)}, u32[]{:S(2)}) copy-start(bf16[22,1,8,3,1440]{4,2,3,1,0:T(8,128)(2,1)} %param.3) | copy-start | bytes 4561924
  27.4 59.6 %all-to-all-start = ((bf16[22,32,8,84]{3,2,0,1:T(8,128)(2,1)}), bf16[22,32,8,84]{3,2,0,1:T(8,128)(2,1)S(1)}, u32[]{:S(2)}, u32[]{:S(2)}) async-start(bf16[22,32,8,84]{3,2,0,1:T(8,128)(2,1)} %copy.174), calls=%async_computation | async-start | bytes 2883584 | tf_op jit(solution)/shard_map/all_to_all | solution.py:72
  106.7 51.8 %collective-permute-start = (bf16[2,8,1,3,14,384]{5,1,4,3,2,0:T(8,128)(2,1)}, bf16[2,8,1,3,14,384]{5,1,4,3,2,0:T(8,128)(2,1)}, u32[]{:S(2)}, u32[]{:S(2)}) collective-permute-start(bf16[2,8,1,3,14,384]{5,1,4,3,2,0:T(8,128)(2,1)} %copy.179), channel_id=1, source_target_pairs={{480,0},{0,32},{32,64},{64,96},{96,128},{128,160},{160,192},{192,2... | collective-permute-start | bytes 1548296 | tf_op jit(solution)/shard_map/ppermute | solution.py:16
  147.4 20.4 %collective-permute-start.2 = (bf16[2,8,1,3,14,384]{5,1,4,3,2,0:T(8,128)(2,1)}, bf16[2,8,1,3,14,384]{5,1,4,3,2,0:T(8,128)(2,1)S(1)}, u32[]{:S(2)}, u32[]{:S(2)}) collective-permute-start(bf16[2,8,1,3,14,384]{5,1,4,3,2,0:T(8,128)(2,1)} %copy.179), channel_id=1, source_target_pairs={{448,0},{480,32},{0,64},{32,96},{64,128},{96,160},{128,192},{160,2... | collective-permute-start | bytes 1548296 | tf_op jit(solution)/shard_map/ppermute | solution.py:16
  149.3 29.6 %collective-permute-start.4 = (bf16[2,8,1,3,14,384]{5,1,4,3,2,0:T(8,128)(2,1)}, bf16[2,8,1,3,14,384]{5,1,4,3,2,0:T(8,128)(2,1)S(1)}, u32[]{:S(2)}, u32[]{:S(2)}) collective-permute-start(bf16[2,8,1,3,14,384]{5,1,4,3,2,0:T(8,128)(2,1)} %copy.179), channel_id=1, source_target_pairs={{416,0},{448,32},{480,64},{0,96},{32,128},{64,160},{96,192},{128,2... | collective-permute-start | bytes 1548296 | tf_op jit(solution)/shard_map/ppermute | solution.py:16
  151.2 101.4 %collective-permute-start.6 = (bf16[2,8,1,3,14,384]{5,1,4,3,2,0:T(8,128)(2,1)}, bf16[2,8,1,3,14,384]{5,1,4,3,2,0:T(8,128)(2,1)S(1)}, u32[]{:S(2)}, u32[]{:S(2)}) collective-permute-start(bf16[2,8,1,3,14,384]{5,1,4,3,2,0:T(8,128)(2,1)} %copy.179), channel_id=1, source_target_pairs={{384,0},{416,32},{448,64},{480,96},{0,128},{32,160},{64,192},{96,2... | collective-permute-start | bytes 1548296 | tf_op jit(solution)/shard_map/ppermute | solution.py:16
  153.2 99.6 %collective-permute-start.8 = (bf16[2,8,1,3,14,384]{5,1,4,3,2,0:T(8,128)(2,1)}, bf16[2,8,1,3,14,384]{5,1,4,3,2,0:T(8,128)(2,1)S(1)}, u32[]{:S(2)}, u32[]{:S(2)}) collective-permute-start(bf16[2,8,1,3,14,384]{5,1,4,3,2,0:T(8,128)(2,1)} %copy.179), channel_id=1, source_target_pairs={{352,0},{384,32},{416,64},{448,96},{480,128},{0,160},{32,192},{64,... | collective-permute-start | bytes 1548296 | tf_op jit(solution)/shard_map/ppermute | solution.py:16
  158.4 154.9 %collective-permute-start.10 = (bf16[2,8,1,3,14,384]{5,1,4,3,2,0:T(8,128)(2,1)}, bf16[2,8,1,3,14,384]{5,1,4,3,2,0:T(8,128)(2,1)S(1)}, u32[]{:S(2)}, u32[]{:S(2)}) collective-permute-start(bf16[2,8,1,3,14,384]{5,1,4,3,2,0:T(8,128)(2,1)} %copy.179), channel_id=1, source_target_pairs={{320,0},{352,32},{384,64},{416,96},{448,128},{480,160},{0,192},{32... | collective-permute-start | bytes 1548296 | tf_op jit(solution)/shard_map/ppermute | solution.py:16
  167.8 145.7 %collective-permute-start.12 = (bf16[2,8,1,3,14,384]{5,1,4,3,2,0:T(8,128)(2,1)}, bf16[2,8,1,3,14,384]{5,1,4,3,2,0:T(8,128)(2,1)S(1)}, u32[]{:S(2)}, u32[]{:S(2)}) collective-permute-start(bf16[2,8,1,3,14,384]{5,1,4,3,2,0:T(8,128)(2,1)} %copy.179), channel_id=1, source_target_pairs={{288,0},{320,32},{352,64},{384,96},{416,128},{448,160},{480,192},{... | collective-permute-start | bytes 1548296 | tf_op jit(solution)/shard_map/ppermute | solution.py:16
  178.9 175.5 %collective-permute-start.14 = (bf16[2,8,1,3,14,384]{5,1,4,3,2,0:T(8,128)(2,1)}, bf16[2,8,1,3,14,384]{5,1,4,3,2,0:T(8,128)(2,1)S(1)}, u32[]{:S(2)}, u32[]{:S(2)}) collective-permute-start(bf16[2,8,1,3,14,384]{5,1,4,3,2,0:T(8,128)(2,1)} %copy.179), channel_id=1, source_target_pairs={{256,0},{288,32},{320,64},{352,96},{384,128},{416,160},{448,192},{... | collective-permute-start | bytes 1548296 | tf_op jit(solution)/shard_map/ppermute | solution.py:16
  358.1 45.2 %collective-permute-start.13 = (f32[2,3,1,1,14,384]{5,4,1,3,2,0:T(8,128)S(1)}, f32[2,3,1,1,14,384]{5,4,1,3,2,0:T(8,128)S(1)}, u32[]{:S(2)}, u32[]{:S(2)}) collective-permute-start(f32[2,3,1,1,14,384]{5,4,1,3,2,0:T(8,128)S(1)} %pad_maximum_fusion.7), channel_id=1, source_target_pairs={{224,0},{256,32},{288,64},{320,96},{352,128},{384,160},{416,192},{... | collective-permute-start | bytes 387080 | tf_op jit(solution)/shard_map/ppermute | solution.py:16
  360.2 43.1 %collective-permute-start.11 = (f32[2,3,1,1,14,384]{5,4,1,3,2,0:T(8,128)S(1)}, f32[2,3,1,1,14,384]{5,4,1,3,2,0:T(8,128)S(1)}, u32[]{:S(2)}, u32[]{:S(2)}) collective-permute-start(f32[2,3,1,1,14,384]{5,4,1,3,2,0:T(8,128)S(1)} %pad_maximum_fusion.6), channel_id=1, source_target_pairs={{192,0},{224,32},{256,64},{288,96},{320,128},{352,160},{384,192},{... | collective-permute-start | bytes 387080 | tf_op jit(solution)/shard_map/ppermute | solution.py:16
  362.2 41.0 %collective-permute-start.9 = (f32[2,3,1,1,14,384]{5,4,1,3,2,0:T(8,128)S(1)}, f32[2,3,1,1,14,384]{5,4,1,3,2,0:T(8,128)S(1)}, u32[]{:S(2)}, u32[]{:S(2)}) collective-permute-start(f32[2,3,1,1,14,384]{5,4,1,3,2,0:T(8,128)S(1)} %pad_maximum_fusion.5), channel_id=1, source_target_pairs={{160,0},{192,32},{224,64},{256,96},{288,128},{320,160},{352,192},{... | collective-permute-start | bytes 387080 | tf_op jit(solution)/shard_map/ppermute | solution.py:16
  366.8 36.2 %collective-permute-start.7 = (f32[2,3,1,1,14,384]{5,4,1,3,2,0:T(8,128)S(1)}, f32[2,3,1,1,14,384]{5,4,1,3,2,0:T(8,128)S(1)}, u32[]{:S(2)}, u32[]{:S(2)}) collective-permute-start(f32[2,3,1,1,14,384]{5,4,1,3,2,0:T(8,128)S(1)} %pad_maximum_fusion.4), channel_id=1, source_target_pairs={{128,0},{160,32},{192,64},{224,96},{256,128},{288,160},{320,192},{... | collective-permute-start | bytes 387080 | tf_op jit(solution)/shard_map/ppermute | solution.py:16
  374.1 7.1 %collective-permute-start.1 = (f32[2,3,1,1,14,384]{5,4,1,3,2,0:T(8,128)S(1)}, f32[2,3,1,1,14,384]{5,4,1,3,2,0:T(8,128)S(1)}, u32[]{:S(2)}, u32[]{:S(2)}) collective-permute-start(f32[2,3,1,1,14,384]{5,4,1,3,2,0:T(8,128)S(1)} %pad_maximum_fusion.1), channel_id=1, source_target_pairs={{32,0},{64,32},{96,64},{128,96},{160,128},{192,160},{224,192},{256... | collective-permute-start | bytes 387080 | tf_op jit(solution)/shard_map/ppermute | solution.py:16
  381.2 11.2 %collective-permute-start.3 = (f32[2,3,1,1,14,384]{5,4,1,3,2,0:T(8,128)S(1)}, f32[2,3,1,1,14,384]{5,4,1,3,2,0:T(8,128)S(1)}, u32[]{:S(2)}, u32[]{:S(2)}) collective-permute-start(f32[2,3,1,1,14,384]{5,4,1,3,2,0:T(8,128)S(1)} %pad_maximum_fusion.2), channel_id=1, source_target_pairs={{64,0},{96,32},{128,64},{160,96},{192,128},{224,160},{256,192},{28... | collective-permute-start | bytes 387080 | tf_op jit(solution)/shard_map/ppermute | solution.py:16
  392.4 10.6 %collective-permute-start.5 = (f32[2,3,1,1,14,384]{5,4,1,3,2,0:T(8,128)S(1)}, f32[2,3,1,1,14,384]{5,4,1,3,2,0:T(8,128)S(1)}, u32[]{:S(2)}, u32[]{:S(2)}) collective-permute-start(f32[2,3,1,1,14,384]{5,4,1,3,2,0:T(8,128)S(1)} %pad_maximum_fusion.3), channel_id=1, source_target_pairs={{96,0},{128,32},{160,64},{192,96},{224,128},{256,160},{288,192},{3... | collective-permute-start | bytes 387080 | tf_op jit(solution)/shard_map/ppermute | solution.py:16
where the time goes:
time: 409 us; the launch traced here: 408 us
  waiting for transfers between devices  227 us (56%)
  starting transfers between devices  116 us (28%)
  local copies, waits for them, and re-layouts  29.1 us (7%)
  other arithmetic  24.9 us (6%)
  matrix products  9.99 us (2%)
    ppermute x15, waiting for transfers between devices, from_behind(): return lax.ppermute(block, axis, route)  194 us
    ppermute x15, starting transfers between devices, from_behind(): return lax.ppermute(block, axis, route)  95.1 us
    all_to_all x1, waiting for transfers between devices, on_device(): lax.all_to_all(zonal_coeff, 'space', split_axis=1, concat_axis=0, tiled=T...  32.8 us
    all_to_all x1, starting transfers between devices, on_device(): lax.all_to_all(zonal_coeff, 'space', split_axis=1, concat_axis=0, tiled=T...  21.1 us
    another operation x2, local copies, waits for them, and re-layouts  15.8 us
    cos x1, other arithmetic, zonal_table(): jnp.cos(angle_rad)  11.7 us
  transfers between devices with their start and end apart: 16, of which 11 were waited for; matrix products, arithmetic and copies ran while one was open for 2% of the time, Pallas kernels for 0%

commit v1 on v0

v1 whole, which is shorter than its diff:
```python
import math

import jax
import jax.numpy as jnp
import numpy as np
from jax import lax
from jax.experimental import pallas as pl
from jax.experimental.pallas import tpu as pltpu
from jax.sharding import Mesh, PartitionSpec as P

LON, LAT, MK, NL = 1440, 704, 448, 384
NV, NS, NLEV = 3, 8, 16
NZ, NH, NX, NY, NC = 8, 2, 4, 4, 2
STRIPS = NX * NH * NY
LATL = LAT // STRIPS
LATP = 24
KL = MK // STRIPS
VS = NV * NS
F32, BF16 = jnp.float32, jnp.bfloat16
X0 = 32
X1 = LON // X0


def zonal_factors():
    wave = np.zeros((NC, NX, NY, 32), np.int64)
    part = np.zeros((NC, NX, NY, 32), np.int64)
    live = np.zeros((NC, NX, NY, 32), np.float64)
    for c in range(NC):
        for x in range(NX):
            for y in range(NY):
                for h in range(NH):
                    for zl in range(7):
                        for u in range(2):
                            col = (h * 7 + zl) * 2 + u
                            wave[c, x, y, col] = KL * (x * 8 + h * 4 + y) + 2 * zl + c
                            part[c, x, y, col] = u
                            live[c, x, y, col] = 1.0
    wave, part, live = wave.reshape(-1), part.reshape(-1), live.reshape(-1)
    step = 2.0 * math.pi / LON
    a = step * ((np.arange(X1)[:, None] * X0 * wave[None]) % LON)
    b = step * ((np.arange(X0)[:, None] * wave[None]) % LON)
    scale = live / math.sqrt(LON)
    p = np.where(part == 0, np.cos(a), -np.sin(a)) * scale
    q = np.where(part == 0, -np.sin(a), -np.cos(a)) * scale
    return [t.astype(np.float32) for t in (p, q, np.cos(b), np.sin(b))]


def merid_factors():
    col = np.arange(2 * NL)
    jt, t, jj = col // 256, (col // 128) % 2, col % 128
    m = jt * 128 + jj - NL // 2
    strips = np.array([x * 8 + h * 4 + y for h in range(NH) for x in range(NX) for y in range(NY)])
    step = 2.0 * math.pi / LAT
    a = step * ((strips[:, None] * LATL * m[None]) % LAT)
    b = step * ((np.arange(LATP)[:, None] * m[None]) % LAT)
    keep = (np.arange(LATP) < LATL).astype(np.float64)[:, None]
    p = np.where(t == 0, np.cos(a), np.sin(a)) / math.sqrt(LAT)
    q = np.where(t == 0, -np.sin(a), np.cos(a)) / math.sqrt(LAT)
    return [v.astype(np.float32) for v in (p, q, np.cos(b) * keep, np.sin(b) * keep)]


ROWS = LATL * VS


def zonal_kernel(fl_hbm, fs_hbm, p_ref, q_ref, cb_ref, sb_ref, out_ref, fl, fs, xs, tab, zs, sem):
    cp1 = pltpu.make_async_copy(fl_hbm, fl, sem.at[0])
    cp2 = pltpu.make_async_copy(fs_hbm, fs, sem.at[1])
    cp1.start()
    cp2.start()

    def gen(i, carry):
        row = p_ref[pl.ds(i, 1), :] * cb_ref[...] + q_ref[pl.ds(i, 1), :] * sb_ref[...]
        tab[pl.ds(pl.multiple_of(i * X0, X0), X0), :] = row.astype(BF16)
        return carry

    lax.fori_loop(0, X1, gen, 0)
    zs[:, ROWS:, :] = jnp.zeros((8, VS * LATP - ROWS, 128), F32)
    cp1.wait()
    cp2.wait()

    def diff(i, carry):
        g = pl.ds(i * 6, 6)
        d = fl[g].astype(F32) - fs[g].astype(F32)
        xs[pl.ds(pl.multiple_of(i * 48, 48), 48), :] = d.reshape(48, LON).astype(BF16)
        return carry

    lax.fori_loop(0, 11, diff, 0)
    for n in range(4):
        w = tab[:, n * 256 : (n + 1) * 256]

        def mm(i, carry):
            r = pl.ds(pl.multiple_of(i * 176, 16), 176)
            z = jnp.dot(xs[r, :], w, preferred_element_type=F32)
            zs[2 * n, r, :] = z[:, :128]
            zs[2 * n + 1, r, :] = z[:, 128:]
            return carry

        lax.fori_loop(0, 3, mm, 0)

    lane = lax.broadcasted_iota(jnp.int32, (LATP, 128), 1)
    hi = lane >= 64
    odd = (lane // 32) % 2 == 1

    def move(d, carry):
        for g in range(6):
            a = [zs[d, pl.ds(4 * g + i, LATP, stride=VS), :] for i in range(4)]
            b = [None] * 4
            for i in range(2):
                b[i] = jnp.where(hi, pltpu.roll(a[i + 2], 64, 1), a[i])
                b[i + 2] = jnp.where(hi, a[i + 2], pltpu.roll(a[i], 64, 1))
            o = [None] * 4
            for j in (0, 2):
                o[j] = jnp.where(odd, pltpu.roll(b[j + 1], 32, 1), b[j])
                o[j + 1] = jnp.where(odd, b[j + 1], pltpu.roll(b[j], 96, 1))
            for j in range(4):
                out_ref[4 * d + j, :, 128 * g : 128 * (g + 1)] = o[j].astype(BF16)
        return carry

    lax.fori_loop(0, 8, move, 0)


def zonal(fl, fs):
    vm = pl.BlockSpec(memory_space=pltpu.VMEM)
    return pl.pallas_call(
        zonal_kernel,
        out_shape=jax.ShapeDtypeStruct((32, LATP, 768), BF16),
        in_specs=[pl.BlockSpec(memory_space=pl.ANY)] * 2 + [vm] * 4,
        out_specs=vm,
        scratch_shapes=[
            pltpu.VMEM((66, 8, LON), BF16),
            pltpu.VMEM((66, 8, LON), BF16),
            pltpu.VMEM((ROWS, LON), BF16),
            pltpu.VMEM((LON, 1024), BF16),
            pltpu.VMEM((8, VS * LATP, 128), F32),
            pltpu.SemaphoreType.DMA((2,)),
        ],
        compiler_params=pltpu.CompilerParams(vmem_limit_bytes=40 << 20),
        name="zonal",
    )(fl, fs, *[jnp.asarray(t) for t in zonal_factors()])


def split_kernel(r_ref, y_ref, w):
    for lev in range(2):

        def turn(g, carry):
            x = r_ref[lev, :, :, pl.ds(pl.multiple_of(g * 128, 128), 128)].astype(F32)
            xt = x.reshape(16 * LATP, 128).T
            for t in range(3):
                w[t, pl.ds(pl.multiple_of(g * 128, 128), 128), :] = xt[:, t * 128 : (t + 1) * 128]
            return carry

        lax.fori_loop(0, 6, turn, 0)

        def pick(kidx, carry):
            slot = (kidx % 7) * 2 + kidx // 7
            for t in range(3):
                rows = [w[t, pl.ds(kidx * 2 + u, VS, stride=32), :] for u in range(2)]
                y_ref[slot, lev * 48 : (lev + 1) * 48, t * 128 : (t + 1) * 128] = jnp.concatenate(rows, 0).astype(BF16)
            return carry

        lax.fori_loop(0, 14, pick, 0)


def split_waves(r):
    vm = pl.BlockSpec(memory_space=pltpu.VMEM)
    return pl.pallas_call(
        split_kernel,
        out_shape=jax.ShapeDtypeStruct((16, 96, 384), BF16),
        in_specs=[vm],
        out_specs=vm,
        scratch_shapes=[pltpu.VMEM((3, 768, 128), F32)],
        compiler_params=pltpu.CompilerParams(vmem_limit_bytes=40 << 20),
        name="split_waves",
    )(r)


def pairs_kernel(r_ref, p_ref, q_ref, cb_ref, sb_ref, out_ref, tab, sre, sim):
    for i in range(STRIPS):
        row = p_ref[i : i + 1, :] * cb_ref[...] + q_ref[i : i + 1, :] * sb_ref[...]
        tab[i * LATP : (i + 1) * LATP, :] = row.astype(BF16)

    for jt in range(3):
        cols = slice(jt * 256, (jt + 1) * 256)
        w0 = tab[: 16 * LATP, cols]
        w1 = tab[16 * LATP :, cols]

        def mm(z, carry):
            a0 = r_ref[pl.ds(z * 2, 2), 0].reshape(192, 384)
            a1 = r_ref[pl.ds(z * 2, 2), 1].reshape(192, 384)
            prod = jnp.dot(a0, w0, preferred_element_type=F32) + jnp.dot(a1, w1, preferred_element_type=F32)
            for l in range(4):
                c0 = prod[l * 48 : l * 48 + 24]
                c1 = prod[l * 48 + 24 : l * 48 + 48]
                re = c0[:, :128] + c1[:, 128:]
                im = c1[:, :128] - c0[:, 128:]
                rows = pl.ds(pl.multiple_of(z * 96 + l * 24, 8), 24)
                sre[jt, rows, :] = re.astype(BF16).astype(F32)
                sim[jt, rows, :] = im.astype(BF16).astype(F32)
            return carry

        lax.fori_loop(0, 4, mm, 0)

    def block(n, carry):
        jt = n // NV
        v = n % NV
        bre = [sre[jt, pl.ds(v * NS + s, NLEV, stride=VS), :] for s in range(NS)]
        bim = [sim[jt, pl.ds(v * NS + s, NLEV, stride=VS), :] for s in range(NS)]

        def one(a, inner):
            base = a * VS + v * NS
            co = jnp.zeros((NLEV, 128), F32)
            qd = jnp.zeros((NLEV, 128), F32)
            for s in range(NS):
                ar = sre[jt, pl.ds(base + s, NLEV, stride=0), :]
                ai = sim[jt, pl.ds(base + s, NLEV, stride=0), :]
                co = co + ar * bre[s] + ai * bim[s]
                qd = qd + ai * bre[s] - ar * bim[s]
            lanes = pl.ds(pl.multiple_of(jt * 128, 128), 128)
            out_ref[a, pl.ds(pl.multiple_of(v * 16, 16), 16), lanes] = (co * (1.0 / NS)).astype(BF16)
            out_ref[a, pl.ds(pl.multiple_of(48 + v * 16, 16), 16), lanes] = (qd * (1.0 / NS)).astype(BF16)
            return inner

        lax.fori_loop(0, NLEV, one, 0)
        return carry

    lax.fori_loop(0, 3 * NV, block, 0)


def pairs(r):
    vm = pl.BlockSpec(memory_space=pltpu.VMEM)
    return pl.pallas_call(
        pairs_kernel,
        out_shape=jax.ShapeDtypeStruct((NLEV, 96, NL), BF16),
        in_specs=[vm] * 5,
        out_specs=vm,
        scratch_shapes=[
            pltpu.VMEM((STRIPS * LATP, 2 * NL), BF16),
            pltpu.VMEM((3, NLEV * VS, 128), F32),
            pltpu.VMEM((3, NLEV * VS, 128), F32),
        ],
        compiler_params=pltpu.CompilerParams(vmem_limit_bytes=40 << 20),
        name="pairs",
    )(r, *[jnp.asarray(t) for t in merid_factors()])


def place_kernel(r_ref, out_ref, buf):
    for k in range(KL):
        for t in range(3):
            tile = r_ref[k, :, t * 128 : (t + 1) * 128].astype(F32)
            buf[t, pl.ds(k, 16, stride=16), :] = tile
    for b in range(16):
        for t in range(3):
            out_ref[0, b, :, t * 128 : (t + 1) * 128] = buf[t, b * 16 : b * 16 + KL, :]


def place(r):
    return pl.pallas_call(
        place_kernel,
        grid=(6,),
        out_shape=jax.ShapeDtypeStruct((6, NLEV, KL, NL), F32),
        in_specs=[pl.BlockSpec((16, 16, NL), lambda i: (0, i, 0))],
        out_specs=pl.BlockSpec((1, NLEV, KL, NL), lambda i: (i, 0, 0, 0)),
        scratch_shapes=[pltpu.VMEM((3, 256, 128), F32)],
        compiler_params=pltpu.CompilerParams(vmem_limit_bytes=40 << 20),
        name="place",
    )(r)


def on_device(fc_long, fc_short):
    fl = jnp.transpose(fc_long[:, 0], (0, 2, 1, 3)).reshape(66, NS, LON)
    fs = jnp.transpose(fc_short[:, 0], (0, 2, 1, 3)).reshape(66, NS, LON)
    z = zonal(fl, fs)
    r = lax.all_to_all(z, ("core", "x", "y"), 0, 0, tiled=True)
    y = split_waves(r.reshape(2, 16, LATP, 768))
    r2 = lax.all_to_all(y, ("zl", "zh"), 0, 0, tiled=True)
    c = pairs(r2.reshape(8, 2, 96, 384))
    r3 = lax.all_to_all(c, ("zl", "core"), 0, 0, tiled=True)
    out = place(r3)
    return out.reshape(2, NV, 1, NLEV, KL, NL)


def solution(mesh):
    fine = Mesh(mesh.devices.reshape(NZ, NC, NX, NH, NY), ("zl", "core", "x", "zh", "y"))
    spec = P(("x", "zh", "y"), ("zl", "core"), None, None, None)
    return jax.shard_map(
        on_device,
        mesh=fine,
        in_specs=(spec, spec),
        out_specs=P(None, None, ("zl", "core"), None, ("x", "zh", "y"), None),
        check_vma=False,
    )
```

time: 409 us -> 191 us (0.47)
  waiting for transfers between devices: 227 us -> 0 us
  blocking collectives: 0 us -> 163 us
  starting transfers between devices: 116 us -> 0 us
  other arithmetic: 24.9 us -> 0 us
  local copies, waits for them, and re-layouts: 29.1 us -> 8.48 us
  Pallas kernels: 0 us -> 18.8 us
  matrix products: 9.99 us -> 0 us
    ppermute x15 -> x0, waiting for transfers between devices: 194 us -> none  [from_behind(): return lax.ppermute(block, axis, route)]
    all_to_all x0 -> x3, blocking collectives: none -> 163 us  [the longest x1 70.1 us: on_device(): r2 = lax.all_to_all(y, ('zl', 'zh'), 0, 0, tiled=True)]
    ppermute x15 -> x0, starting transfers between devices: 95.1 us -> none  [from_behind(): return lax.ppermute(block, axis, route)]
    all_to_all x1 -> x0, waiting for transfers between devices: 32.8 us -> none  [on_device(): lax.all_to_all(zonal_coeff, 'space', split_axis=1, concat_axis=0, tiled=T...]
    all_to_all x1 -> x0, starting transfers between devices: 21.1 us -> none  [on_device(): lax.all_to_all(zonal_coeff, 'space', split_axis=1, concat_axis=0, tiled=T...]
    pallas_call x0 -> x4, Pallas kernels: none -> 18.8 us  [the longest x1 7.61 us: pairs(): pl.pallas_call(pairs_kernel, out_shape=jax.ShapeDtypeStruct((NLEV, 96, NL...]
    cos x2 -> x0, other arithmetic: 17.5 us -> none  [the longest x1 11.7 us: zonal_table(): jnp.cos(angle_rad)]
    another operation x9 -> x0, local copies, waits for them, and re-layouts: 17 us -> none
  transfers between devices with their start and end apart: 16 -> 0, of which waited for: 11 -> 0; matrix products, arithmetic and copies ran while one was open for 2% -> 0% of each run, Pallas kernels for 0% -> 0%
where the time goes in v1:
time: 191 us; the launch traced here: 190 us
  blocking collectives  163 us (85%)
  Pallas kernels  18.8 us (10%)
  local copies, waits for them, and re-layouts  8.48 us (4%)
    all_to_all x1, blocking collectives, on_device(): r2 = lax.all_to_all(y, ('zl', 'zh'), 0, 0, tiled=True)  70.1 us
    all_to_all x1, blocking collectives, on_device(): r3 = lax.all_to_all(c, ('zl', 'core'), 0, 0, tiled=True)  64.4 us
    all_to_all x1, blocking collectives, on_device(): r = lax.all_to_all(z, ('core', 'x', 'y'), 0, 0, tiled=True)  28.4 us
    pallas_call x1, Pallas kernels, pairs(): pl.pallas_call(pairs_kernel, out_shape=jax.ShapeDtypeStruct((NLEV, 96, NL...  7.61 us
    pallas_call x1, Pallas kernels, zonal(): pl.pallas_call(zonal_kernel, out_shape=jax.ShapeDtypeStruct((32, LATP, 76...  7.18 us
    unnamed x20, local copies, waits for them, and re-layouts  6.54 us

profile of v1, /device:TPU:1, one launch (start us, length us, event | category | flops | bytes accessed | tf_op | source)
XLA Modules:
  0.0 190.3 jit_solution(4467629223594789074)
XLA Ops:
  0.0 0.0 copy-start
  0.0 1.4 copy-done
  1.4 0.0 copy-start.1
  1.4 1.4 copy-done.1
  2.9 0.0 copy-start.2
  2.9 0.9 copy-done.2
  3.8 0.0 copy-start.3
  3.8 0.9 copy-done.3
  4.7 0.0 copy-start.4
  4.7 0.9 copy-done.4
  5.6 0.0 copy-start.5
  5.6 0.9 copy-done.5
  6.5 7.2 %zonal.1 = bf16[32,24,768]{2,1,0:T(8,128)(2,1)S(1)} custom-call(bf16[66,8,1440]{2,1,0:T(8,128)(2,1)S(1)} %bitcast.16, bf16[66,8,1440]{2,1,0:T(8,128)(2,1)S(1)} %bitcast.17, f32[45,1024]{1,0:T(8,128)S(1)} %copy-done.3, f32[45,1024]{1,0:T(8,128)S(1)} %copy-done.2, f32[32,1024]{1,0:T(8,128)S(1)} %copy-done.5, f32[32,1024]{1,0:T(8,128)S(1)} %copy-done.4), custom_call_target="tpu_custom_call" | custom-call | tf_op jit(solution)/shard_map/zonal/pallas_call | solution.py:124
  13.7 28.4 %all_to_all.15 = bf16[32,24,768]{2,1,0:T(8,128)(2,1)S(1)} all-to-all(bf16[32,24,768]{2,1,0:T(8,128)(2,1)S(1)} %zonal.1), channel_id=1, replica_groups=mesh['zl'=8,'core'=2,'x'=4,'zh'=2,'y'=4] {'core','x','y'}, dimensions={0} | all-to-all | bytes 2359296 | tf_op jit(solution)/shard_map/all_to_all | solution.py:273
  42.2 2.7 %split_waves.1 = bf16[16,96,384]{2,1,0:T(8,128)(2,1)S(1)} custom-call(bf16[2,16,24,768]{3,2,1,0:T(8,128)(2,1)S(1)} %bitcast.14), custom_call_target="tpu_custom_call" | custom-call | tf_op jit(solution)/shard_map/split_waves/pallas_call | solution.py:166
  44.9 0.0 copy-start.6
  44.9 0.0 copy-start.7
  44.9 0.0 copy-start.8
  44.9 0.0 copy-start.9
  44.9 70.1 %all_to_all.16 = bf16[16,96,384]{2,1,0:T(8,128)(2,1)S(1)} all-to-all(bf16[16,96,384]{2,1,0:T(8,128)(2,1)S(1)} %split_waves.1), channel_id=1, replica_groups=mesh['zl'=8,'core'=2,'x'=4,'zh'=2,'y'=4] {'zl','zh'}, dimensions={0} | all-to-all | bytes 2359296 | tf_op jit(solution)/shard_map/all_to_all | solution.py:275
  115.0 0.0 copy-done.6
  115.0 0.0 copy-done.7
  115.0 0.0 copy-done.8
  115.0 0.0 copy-done.9
  115.0 7.6 %pairs.1 = bf16[16,96,384]{2,1,0:T(8,128)(2,1)S(1)} custom-call(bf16[8,2,96,384]{3,2,1,0:T(8,128)(2,1)S(1)} %bitcast.15, f32[32,768]{1,0:T(8,128)S(1)} %copy-done.7, f32[32,768]{1,0:T(8,128)S(1)} %copy-done.6, f32[24,768]{1,0:T(8,128)S(1)} %copy-done.9, f32[24,768]{1,0:T(8,128)S(1)} %copy-done.8), custom_call_target="tpu_custom_call" | custom-call | tf_op jit(solution)/shard_map/pairs/pallas_call | solution.py:231
  122.6 64.4 %all_to_all.17.r_ref = bf16[16,96,384]{2,1,0:T(8,128)(2,1)S(1)} all-to-all(bf16[16,96,384]{2,1,0:T(8,128)(2,1)S(1)} %pairs.1), channel_id=1, replica_groups=mesh['zl'=8,'core'=2,'x'=4,'zh'=2,'y'=4] {'zl','core'}, dimensions={0} | all-to-all | bytes 2359296 | tf_op jit(solution)/shard_map/all_to_all | solution.py:277
  187.1 1.3 place.1
  188.4 1.9 %copy.11 = f32[2,3,1,16,14,384]{5,3,4,2,1,0:T(8,128)} copy(f32[2,3,1,16,14,384]{5,4,3,1,0,2:T(8,128)S(1)} %bitcast.13) | data formatting | bytes 4128768 | tf_op jit(solution)/shard_map/reshape | solution.py:279
Async XLA Ops:
  0.0 1.4 copy-start
  1.4 1.4 copy-start.1
  2.9 0.9 copy-start.2
  3.8 0.9 copy-start.3
  4.7 0.9 copy-start.4
  5.6 0.9 copy-start.5
  44.9 70.1 %copy-start.6 = (f32[32,768]{1,0:T(8,128)S(1)}, f32[32,768]{1,0:T(8,128)}, u32[]{:S(2)}) copy-start(f32[32,768]{1,0:T(8,128)} %constant.21.clone.q_ref) | copy-start | bytes 294916
  44.9 70.1 %copy-start.7 = (f32[32,768]{1,0:T(8,128)S(1)}, f32[32,768]{1,0:T(8,128)}, u32[]{:S(2)}) copy-start(f32[32,768]{1,0:T(8,128)} %constant.20.clone.p_ref) | copy-start | bytes 294916
  44.9 70.1 %copy-start.8 = (f32[24,768]{1,0:T(8,128)S(1)}, f32[24,768]{1,0:T(8,128)}, u32[]{:S(2)}) copy-start(f32[24,768]{1,0:T(8,128)} %constant.23.clone.sb_ref) | copy-start | bytes 221188
  44.9 70.1 %copy-start.9 = (f32[24,768]{1,0:T(8,128)S(1)}, f32[24,768]{1,0:T(8,128)}, u32[]{:S(2)}) copy-start(f32[24,768]{1,0:T(8,128)} %constant.22.clone.cb_ref) | copy-start | bytes 221188

commit v2 on v1

--- a/solution.py
+++ b/solution.py
@@ -62,19 +62,22 @@
 ROWS = LATL * VS
 
 
-def zonal_kernel(fl_hbm, fs_hbm, p_ref, q_ref, cb_ref, sb_ref, out_ref, fl, fs, xs, tab, zs, sem):
-    cp1 = pltpu.make_async_copy(fl_hbm, fl, sem.at[0])
-    cp2 = pltpu.make_async_copy(fs_hbm, fs, sem.at[1])
+def zonal_kernel(fl_hbm, fs_hbm, f_hbm, out_ref, fl, fs, fac, xs, tab, zs, sem):
+    cp0 = pltpu.make_async_copy(f_hbm, fac, sem.at[0])
+    cp1 = pltpu.make_async_copy(fl_hbm, fl, sem.at[1])
+    cp2 = pltpu.make_async_copy(fs_hbm, fs, sem.at[2])
+    cp0.start()
     cp1.start()
     cp2.start()
+    zs[:, ROWS:, :] = jnp.zeros((8, VS * LATP - ROWS, 128), F32)
+    cp0.wait()
 
     def gen(i, carry):
-        row = p_ref[pl.ds(i, 1), :] * cb_ref[...] + q_ref[pl.ds(i, 1), :] * sb_ref[...]
+        row = fac[pl.ds(i, 1), :] * fac[96:128, :] + fac[pl.ds(48 + i, 1), :] * fac[128:160, :]
         tab[pl.ds(pl.multiple_of(i * X0, X0), X0), :] = row.astype(BF16)
         return carry
 
     lax.fori_loop(0, X1, gen, 0)
-    zs[:, ROWS:, :] = jnp.zeros((8, VS * LATP - ROWS, 128), F32)
     cp1.wait()
     cp2.wait()
 
@@ -85,17 +88,15 @@
         return carry
 
     lax.fori_loop(0, 11, diff, 0)
-    for n in range(4):
-        w = tab[:, n * 256 : (n + 1) * 256]
-
-        def mm(i, carry):
-            r = pl.ds(pl.multiple_of(i * 176, 16), 176)
-            z = jnp.dot(xs[r, :], w, preferred_element_type=F32)
-            zs[2 * n, r, :] = z[:, :128]
-            zs[2 * n + 1, r, :] = z[:, 128:]
-            return carry
-
-        lax.fori_loop(0, 3, mm, 0)
+
+    def mm(n, carry):
+        w = tab[:, pl.ds(pl.multiple_of(n * 256, 256), 256)]
+        z = jnp.dot(xs[...], w, preferred_element_type=F32)
+        zs[2 * n, :ROWS, :] = z[:, :128]
+        zs[2 * n + 1, :ROWS, :] = z[:, 128:]
+        return carry
+
+    lax.fori_loop(0, 4, mm, 0)
 
     lane = lax.broadcasted_iota(jnp.int32, (LATP, 128), 1)
     hi = lane >= 64
@@ -120,23 +121,26 @@
 
 
 def zonal(fl, fs):
-    vm = pl.BlockSpec(memory_space=pltpu.VMEM)
+    p, q, cb, sb = zonal_factors()
+    fac = np.zeros((160, 1024), np.float32)
+    fac[:X1], fac[48 : 48 + X1], fac[96:128], fac[128:] = p, q, cb, sb
+    hbm = pl.BlockSpec(memory_space=pltpu.HBM)
     return pl.pallas_call(
         zonal_kernel,
         out_shape=jax.ShapeDtypeStruct((32, LATP, 768), BF16),
-        in_specs=[pl.BlockSpec(memory_space=pl.ANY)] * 2 + [vm] * 4,
-        out_specs=vm,
+        in_specs=[hbm] * 3,
+        out_specs=pl.BlockSpec(memory_space=pltpu.VMEM),
         scratch_shapes=[
             pltpu.VMEM((66, 8, LON), BF16),
             pltpu.VMEM((66, 8, LON), BF16),
+            pltpu.VMEM((160, 1024), F32),
             pltpu.VMEM((ROWS, LON), BF16),
             pltpu.VMEM((LON, 1024), BF16),
             pltpu.VMEM((8, VS * LATP, 128), F32),
-            pltpu.SemaphoreType.DMA((2,)),
+            pltpu.SemaphoreType.DMA((3,)),
         ],
-        compiler_params=pltpu.CompilerParams(vmem_limit_bytes=40 << 20),
         name="zonal",
-    )(fl, fs, *[jnp.asarray(t) for t in zonal_factors()])
+    )(fl, fs, jnp.asarray(fac))
 
 
 def split_kernel(r_ref, y_ref, w):
@@ -174,31 +178,41 @@
     )(r)
 
 
-def pairs_kernel(r_ref, p_ref, q_ref, cb_ref, sb_ref, out_ref, tab, sre, sim):
+def table_kernel(f_ref, tab):
     for i in range(STRIPS):
-        row = p_ref[i : i + 1, :] * cb_ref[...] + q_ref[i : i + 1, :] * sb_ref[...]
+        row = f_ref[i : i + 1, :] * f_ref[64:88, :] + f_ref[32 + i : 33 + i, :] * f_ref[88:112, :]
         tab[i * LATP : (i + 1) * LATP, :] = row.astype(BF16)
 
-    for jt in range(3):
-        cols = slice(jt * 256, (jt + 1) * 256)
-        w0 = tab[: 16 * LATP, cols]
-        w1 = tab[16 * LATP :, cols]
-
-        def mm(z, carry):
-            a0 = r_ref[pl.ds(z * 2, 2), 0].reshape(192, 384)
-            a1 = r_ref[pl.ds(z * 2, 2), 1].reshape(192, 384)
-            prod = jnp.dot(a0, w0, preferred_element_type=F32) + jnp.dot(a1, w1, preferred_element_type=F32)
-            for l in range(4):
-                c0 = prod[l * 48 : l * 48 + 24]
-                c1 = prod[l * 48 + 24 : l * 48 + 48]
-                re = c0[:, :128] + c1[:, 128:]
-                im = c1[:, :128] - c0[:, 128:]
-                rows = pl.ds(pl.multiple_of(z * 96 + l * 24, 8), 24)
-                sre[jt, rows, :] = re.astype(BF16).astype(F32)
-                sim[jt, rows, :] = im.astype(BF16).astype(F32)
-            return carry
-
-        lax.fori_loop(0, 4, mm, 0)
+
+def merid_table():
+    vm = pl.BlockSpec(memory_space=pltpu.VMEM)
+    return pl.pallas_call(
+        table_kernel,
+        out_shape=jax.ShapeDtypeStruct((STRIPS * LATP, 2 * NL), BF16),
+        in_specs=[vm],
+        out_specs=vm,
+        cost_estimate=pl.CostEstimate(flops=3 * 768 * 768, bytes_accessed=1600000, transcendentals=0),
+        compiler_params=pltpu.CompilerParams(vmem_limit_bytes=8 << 20),
+        name="merid_table",
+    )(jnp.asarray(np.concatenate(merid_factors(), 0)))
+
+
+def pairs_kernel(r_ref, tab, out_ref, sre, sim):
+    a0 = r_ref[:, 0].reshape(768, 384)
+    a1 = r_ref[:, 1].reshape(768, 384)
+
+    def merid(jt, carry):
+        cols = pl.ds(pl.multiple_of(jt * 256, 256), 256)
+        prod = jnp.dot(a0, tab[: 16 * LATP, cols], preferred_element_type=F32)
+        prod = prod + jnp.dot(a1, tab[16 * LATP :, cols], preferred_element_type=F32)
+        for l in range(NLEV):
+            c0 = prod[l * 48 : l * 48 + 24]
+            c1 = prod[l * 48 + 24 : l * 48 + 48]
+            sre[jt, l * 24 : (l + 1) * 24, :] = (c0[:, :128] + c1[:, 128:]).astype(BF16).astype(F32)
+            sim[jt, l * 24 : (l + 1) * 24, :] = (c1[:, :128] - c0[:, 128:]).astype(BF16).astype(F32)
+        return carry
+
+    lax.fori_loop(0, 3, merid, 0)
 
     def block(n, carry):
         jt = n // NV
@@ -226,42 +240,34 @@
     lax.fori_loop(0, 3 * NV, block, 0)
 
 
-def pairs(r):
+def pairs(r, tab):
     vm = pl.BlockSpec(memory_space=pltpu.VMEM)
     return pl.pallas_call(
         pairs_kernel,
         out_shape=jax.ShapeDtypeStruct((NLEV, 96, NL), BF16),
-        in_specs=[vm] * 5,
+        in_specs=[vm] * 2,
         out_specs=vm,
         scratch_shapes=[
-            pltpu.VMEM((STRIPS * LATP, 2 * NL), BF16),
             pltpu.VMEM((3, NLEV * VS, 128), F32),
             pltpu.VMEM((3, NLEV * VS, 128), F32),
         ],
         compiler_params=pltpu.CompilerParams(vmem_limit_bytes=40 << 20),
         name="pairs",
-    )(r, *[jnp.asarray(t) for t in merid_factors()])
-
-
-def place_kernel(r_ref, out_ref, buf):
+    )(r, tab)
+
+
+def place_kernel(r_ref, out_ref):
     for k in range(KL):
-        for t in range(3):
-            tile = r_ref[k, :, t * 128 : (t + 1) * 128].astype(F32)
-            buf[t, pl.ds(k, 16, stride=16), :] = tile
-    for b in range(16):
-        for t in range(3):
-            out_ref[0, b, :, t * 128 : (t + 1) * 128] = buf[t, b * 16 : b * 16 + KL, :]
+        out_ref[0, k] = r_ref[k].astype(F32)
 
 
 def place(r):
     return pl.pallas_call(
         place_kernel,
         grid=(6,),
-        out_shape=jax.ShapeDtypeStruct((6, NLEV, KL, NL), F32),
+        out_shape=jax.ShapeDtypeStruct((6, KL, NLEV, NL), F32),
         in_specs=[pl.BlockSpec((16, 16, NL), lambda i: (0, i, 0))],
-        out_specs=pl.BlockSpec((1, NLEV, KL, NL), lambda i: (i, 0, 0, 0)),
-        scratch_shapes=[pltpu.VMEM((3, 256, 128), F32)],
-        compiler_params=pltpu.CompilerParams(vmem_limit_bytes=40 << 20),
+        out_specs=pl.BlockSpec((1, KL, NLEV, NL), lambda i: (i, 0, 0, 0)),
         name="place",
     )(r)
 
@@ -273,10 +279,11 @@
     r = lax.all_to_all(z, ("core", "x", "y"), 0, 0, tiled=True)
     y = split_waves(r.reshape(2, 16, LATP, 768))
     r2 = lax.all_to_all(y, ("zl", "zh"), 0, 0, tiled=True)
-    c = pairs(r2.reshape(8, 2, 96, 384))
+    c = pairs(r2.reshape(8, 2, 96, 384), merid_table())
     r3 = lax.all_to_all(c, ("zl", "core"), 0, 0, tiled=True)
     out = place(r3)
-    return out.reshape(2, NV, 1, NLEV, KL, NL)
+    out = out.reshape(2, NV, 1, KL, NLEV, NL)
+    return jnp.swapaxes(out, 3, 4)
 
 
 def solution(mesh):

time: 191 us -> 186 us (0.974)
  blocking collectives: 163 us -> 93.3 us
  waiting for transfers between devices: 0 us -> 56.7 us
  starting transfers between devices: 0 us -> 13.1 us
  local copies, waits for them, and re-layouts: 8.48 us -> 0.01 us
  Pallas kernels: 18.8 us -> 22.2 us
    all_to_all x1 -> x0, blocking collectives: 70.1 us -> none  [on_device(): r2 = lax.all_to_all(y, ('zl', 'zh'), 0, 0, tiled=True)]
    all_to_all x0 -> x1, waiting for transfers between devices: none -> 56.7 us  [on_device(): r2 = lax.all_to_all(y, ('zl', 'zh'), 0, 0, tiled=True)]
    all_to_all x0 -> x1, starting transfers between devices: none -> 13.1 us  [on_device(): r2 = lax.all_to_all(y, ('zl', 'zh'), 0, 0, tiled=True)]
    unnamed x20 -> x2, local copies, waits for them, and re-layouts: 6.54 us -> 0.01 us
    pallas_call x1, Pallas kernels: 1.32 us -> 4.6 us  [place(): pl.pallas_call(place_kernel, grid=(6,), out_shape=jax.ShapeDtypeStruct((6...]
    reshape x1 -> x0, local copies, waits for them, and re-layouts: 1.95 us -> none  [on_device(): return out.reshape(2, NV, 1, NLEV, KL, NL)]
  transfers between devices with their start and end apart: 0 -> 1, of which waited for: 0 -> 1; matrix products, arithmetic and copies ran while one was open for 0% -> 0% of each run, Pallas kernels for 0% -> 0%
where the time goes in v2:
time: 186 us; the launch traced here: 185 us
  blocking collectives  93.3 us (50%)
  waiting for transfers between devices  56.7 us (30%)
  Pallas kernels  22.2 us (12%)
  starting transfers between devices  13.1 us (7%)
    all_to_all x1, blocking collectives, on_device(): r3 = lax.all_to_all(c, ('zl', 'core'), 0, 0, tiled=True)  63.9 us
    all_to_all x1, waiting for transfers between devices, on_device(): r2 = lax.all_to_all(y, ('zl', 'zh'), 0, 0, tiled=True)  56.7 us
    all_to_all x1, blocking collectives, on_device(): r = lax.all_to_all(z, ('core', 'x', 'y'), 0, 0, tiled=True)  29.4 us
    all_to_all x1, starting transfers between devices, on_device(): r2 = lax.all_to_all(y, ('zl', 'zh'), 0, 0, tiled=True)  13.1 us
    pallas_call x1, Pallas kernels, zonal(): pl.pallas_call(zonal_kernel, out_shape=jax.ShapeDtypeStruct((32, LATP, 76...  7.56 us
    pallas_call x1, Pallas kernels, pairs(): pl.pallas_call(pairs_kernel, out_shape=jax.ShapeDtypeStruct((NLEV, 96, NL...  5.98 us
    pallas_call x1, Pallas kernels, place(): pl.pallas_call(place_kernel, grid=(6,), out_shape=jax.ShapeDtypeStruct((6...  4.6 us
    pallas_call x1, Pallas kernels, split_waves(): pl.pallas_call(split_kernel, out_shape=jax.ShapeDtypeStruct((16, 96, 384)...  3.73 us
  transfers between devices with their start and end apart: 1, of which 1 were waited for; matrix products, arithmetic and copies ran while one was open for 0% of the time, Pallas kernels for 0%

profile of v2, /device:TPU:1, one launch (start us, length us, event | category | flops | bytes accessed | tf_op | source)
XLA Modules:
  0.0 185.4 jit_solution(824966447603116388)
XLA Ops:
  0.0 7.6 %zonal.1 = bf16[32,24,768]{2,1,0:T(8,128)(2,1)} custom-call(bf16[66,8,1440]{2,1,0:T(8,128)(2,1)} %bitcast.19, bf16[66,8,1440]{2,1,0:T(8,128)(2,1)} %bitcast.20, f32[160,1024]{1,0:T(8,128)} %constant.4.clone.f_hbm), custom_call_target="tpu_custom_call" | custom-call | tf_op jit(solution)/shard_map/zonal/pallas_call | solution.py:128
  7.6 29.4 %all_to_all.15 = bf16[32,24,768]{2,1,0:T(8,128)(2,1)S(1)} all-to-all(bf16[32,24,768]{2,1,0:T(8,128)(2,1)} %zonal.1), channel_id=1, replica_groups=mesh['zl'=8,'core'=2,'x'=4,'zh'=2,'y'=4] {'core','x','y'}, dimensions={0} | all-to-all | bytes 2359296 | tf_op jit(solution)/shard_map/all_to_all | solution.py:279
  37.0 3.7 %split_waves.1 = bf16[16,96,384]{2,1,0:T(8,128)(2,1)} custom-call(bf16[2,16,24,768]{3,2,1,0:T(8,128)(2,1)S(1)} %bitcast.18), custom_call_target="tpu_custom_call" | custom-call | tf_op jit(solution)/shard_map/split_waves/pallas_call | solution.py:170
  40.7 0.0 copy-start
  40.7 13.1 %all-to-all-start.1 = ((bf16[16,96,384]{2,1,0:T(8,128)(2,1)}), bf16[16,96,384]{2,1,0:T(8,128)(2,1)S(1)}, u32[]{:S(2)}, u32[]{:S(2)}) async-start(bf16[16,96,384]{2,1,0:T(8,128)(2,1)} %split_waves.1), calls=%async_computation.1 | async-start | bytes 2359296 | tf_op jit(solution)/shard_map/all_to_all | solution.py:281
  53.8 0.0 copy-done
  53.8 0.3 merid_table.1.tab
  54.1 56.7 %all-to-all-done.1 = bf16[16,96,384]{2,1,0:T(8,128)(2,1)S(1)} async-done(((bf16[16,96,384]{2,1,0:T(8,128)(2,1)}), bf16[16,96,384]{2,1,0:T(8,128)(2,1)S(1)}, u32[]{:S(2)}, u32[]{:S(2)}) %all-to-all-start.1) | async-done | bytes 1179680 | tf_op jit(solution)/shard_map/all_to_all | solution.py:281
  110.8 6.0 %pairs.1 = bf16[16,96,384]{2,1,0:T(8,128)(2,1)S(1)} custom-call(bf16[8,2,96,384]{3,2,1,0:T(8,128)(2,1)S(1)} %bitcast.17, bf16[768,768]{1,0:T(8,128)(2,1)S(1)} %merid_table.1.tab), custom_call_target="tpu_custom_call" | custom-call | tf_op jit(solution)/shard_map/pairs/pallas_call | solution.py:245
  116.8 63.9 %all_to_all.16.r_ref = bf16[16,96,384]{2,1,0:T(8,128)(2,1)} all-to-all(bf16[16,96,384]{2,1,0:T(8,128)(2,1)S(1)} %pairs.1), channel_id=1, replica_groups=mesh['zl'=8,'core'=2,'x'=4,'zh'=2,'y'=4] {'zl','core'}, dimensions={0} | all-to-all | bytes 2359296 | tf_op jit(solution)/shard_map/all_to_all | solution.py:283
  180.8 4.6 %place.1 = f32[6,14,16,384]{3,2,1,0:T(8,128)} custom-call(bf16[16,96,384]{2,1,0:T(8,128)(2,1)} %all_to_all.16.r_ref), custom_call_target="tpu_custom_call" | custom-call | tf_op jit(solution)/shard_map/place/pallas_call | solution.py:265
Async XLA Ops:
  40.7 13.1 %copy-start = (f32[112,768]{1,0:T(8,128)S(1)}, f32[112,768]{1,0:T(8,128)}, u32[]{:S(2)}) copy-start(f32[112,768]{1,0:T(8,128)} %constant.5.clone.f_ref) | copy-start | bytes 1032196
  40.7 70.1 %all-to-all-start.1 = ((bf16[16,96,384]{2,1,0:T(8,128)(2,1)}), bf16[16,96,384]{2,1,0:T(8,128)(2,1)S(1)}, u32[]{:S(2)}, u32[]{:S(2)}) async-start(bf16[16,96,384]{2,1,0:T(8,128)(2,1)} %split_waves.1), calls=%async_computation.1 | async-start | bytes 2359296 | tf_op jit(solution)/shard_map/all_to_all | solution.py:281

commit v3 on v2

--- a/solution.py
+++ b/solution.py
@@ -45,18 +45,17 @@
     return [t.astype(np.float32) for t in (p, q, np.cos(b), np.sin(b))]
 
 
-def merid_factors():
+def merid_table():
     col = np.arange(2 * NL)
     jt, t, jj = col // 256, (col // 128) % 2, col % 128
     m = jt * 128 + jj - NL // 2
-    strips = np.array([x * 8 + h * 4 + y for h in range(NH) for x in range(NX) for y in range(NY)])
-    step = 2.0 * math.pi / LAT
-    a = step * ((strips[:, None] * LATL * m[None]) % LAT)
-    b = step * ((np.arange(LATP)[:, None] * m[None]) % LAT)
-    keep = (np.arange(LATP) < LATL).astype(np.float64)[:, None]
-    p = np.where(t == 0, np.cos(a), np.sin(a)) / math.sqrt(LAT)
-    q = np.where(t == 0, -np.sin(a), np.cos(a)) / math.sqrt(LAT)
-    return [v.astype(np.float32) for v in (p, q, np.cos(b) * keep, np.sin(b) * keep)]
+    out = np.zeros((NH, 384, 2 * NL), np.float64)
+    for h in range(NH):
+        strips = np.array([x * 8 + h * 4 + y for x in range(NX) for y in range(NY)])
+        lats = (strips[:, None] * LATL + np.arange(LATL)[None]).reshape(-1)
+        angle = 2.0 * math.pi / LAT * ((lats[:, None] * m[None]) % LAT)
+        out[h, : lats.size] = np.where(t == 0, np.cos(angle), np.sin(angle)) / math.sqrt(LAT)
+    return jnp.asarray(out.reshape(NH * 384, 2 * NL).astype(np.float32)).astype(BF16)
 
 
 ROWS = LATL * VS
@@ -143,68 +142,78 @@
     )(fl, fs, jnp.asarray(fac))
 
 
-def split_kernel(r_ref, y_ref, w):
+SLOT = 264
+
+
+def split_kernel(r_ref, y_ref, pack, w):
     for lev in range(2):
 
         def turn(g, carry):
-            x = r_ref[lev, :, :, pl.ds(pl.multiple_of(g * 128, 128), 128)].astype(F32)
-            xt = x.reshape(16 * LATP, 128).T
-            for t in range(3):
-                w[t, pl.ds(pl.multiple_of(g * 128, 128), 128), :] = xt[:, t * 128 : (t + 1) * 128]
+            lanes = pl.ds(pl.multiple_of(g * 128, 128), 128)
+            for i in range(16):
+                pack[i * LATL : (i + 1) * LATL, :] = r_ref[lev, i, :LATL, lanes].astype(F32)
+            xt = pack[...].T
+            rows = pl.ds(pl.multiple_of(g * 128, 128), 128)
+            w[lev, 0, rows, :] = xt[:, :128]
+            w[lev, 1, rows, :] = xt[:, 128:256]
+            w[lev, 2, rows, :] = xt[:, 256:384]
             return carry
 
         lax.fori_loop(0, 6, turn, 0)
-
-        def pick(kidx, carry):
-            slot = (kidx % 7) * 2 + kidx // 7
-            for t in range(3):
-                rows = [w[t, pl.ds(kidx * 2 + u, VS, stride=32), :] for u in range(2)]
-                y_ref[slot, lev * 48 : (lev + 1) * 48, t * 128 : (t + 1) * 128] = jnp.concatenate(rows, 0).astype(BF16)
-            return carry
-
-        lax.fori_loop(0, 14, pick, 0)
+    tail = lax.broadcasted_iota(jnp.int32, (VS, 128), 1) >= 96
+
+    def pick(kidx, carry):
+        slot = (kidx % 7) * 2 + kidx // 7
+        combos = [(lev, u) for lev in range(2) for u in range(2)]
+        for t in range(2):
+            rows = [w[lev, t, pl.ds(kidx * 2 + u, VS, stride=32), :] for lev, u in combos]
+            y_ref[slot, t * 96 : (t + 1) * 96, :] = jnp.concatenate(rows, 0).astype(BF16)
+        rows = [w[lev, 2, pl.ds(kidx * 2 + u, VS, stride=32), :] for lev, u in combos]
+        mixed = [jnp.where(tail, pltpu.roll(rows[3], 96 - 32 * c, 1), rows[c]) for c in range(3)]
+        y_ref[slot, 192:SLOT, :] = jnp.concatenate(mixed, 0).astype(BF16)
+        return carry
+
+    lax.fori_loop(0, 14, pick, 0)
+    y_ref[14, :, :] = jnp.zeros((SLOT, 128), BF16)
+    y_ref[15, :, :] = jnp.zeros((SLOT, 128), BF16)
 
 
 def split_waves(r):
     vm = pl.BlockSpec(memory_space=pltpu.VMEM)
     return pl.pallas_call(
         split_kernel,
-        out_shape=jax.ShapeDtypeStruct((16, 96, 384), BF16),
+        out_shape=jax.ShapeDtypeStruct((16, SLOT, 128), BF16),
         in_specs=[vm],
         out_specs=vm,
-        scratch_shapes=[pltpu.VMEM((3, 768, 128), F32)],
+        scratch_shapes=[pltpu.VMEM((384, 128), F32), pltpu.VMEM((2, 3, 768, 128), F32)],
         compiler_params=pltpu.CompilerParams(vmem_limit_bytes=40 << 20),
         name="split_waves",
     )(r)
 
 
-def table_kernel(f_ref, tab):
-    for i in range(STRIPS):
-        row = f_ref[i : i + 1, :] * f_ref[64:88, :] + f_ref[32 + i : 33 + i, :] * f_ref[88:112, :]
-        tab[i * LATP : (i + 1) * LATP, :] = row.astype(BF16)
-
-
-def merid_table():
-    vm = pl.BlockSpec(memory_space=pltpu.VMEM)
-    return pl.pallas_call(
-        table_kernel,
-        out_shape=jax.ShapeDtypeStruct((STRIPS * LATP, 2 * NL), BF16),
-        in_specs=[vm],
-        out_specs=vm,
-        cost_estimate=pl.CostEstimate(flops=3 * 768 * 768, bytes_accessed=1600000, transcendentals=0),
-        compiler_params=pltpu.CompilerParams(vmem_limit_bytes=8 << 20),
-        name="merid_table",
-    )(jnp.asarray(np.concatenate(merid_factors(), 0)))
-
-
-def pairs_kernel(r_ref, tab, out_ref, sre, sim):
-    a0 = r_ref[:, 0].reshape(768, 384)
-    a1 = r_ref[:, 1].reshape(768, 384)
+def pairs_kernel(r_ref, tab, out_ref, a_ref, sre, sim):
+    tail = lax.broadcasted_iota(jnp.int32, (VS, 128), 1)
+
+    def unpack(z, carry):
+        rows = pl.ds(pl.multiple_of(z * 96, 32), 96)
+        for h in range(NH):
+            a_ref[h, rows, 0:128] = r_ref[z, h, 0:96, :]
+            a_ref[h, rows, 128:256] = r_ref[z, h, 96:192, :]
+            mixed = [r_ref[z, h, 192 + VS * c : 192 + VS * (c + 1), :].astype(F32) for c in range(3)]
+            last = pltpu.roll(mixed[0], 32, 1)
+            last = jnp.where(tail >= 32, pltpu.roll(mixed[1], 64, 1), last)
+            last = jnp.where(tail >= 64, pltpu.roll(mixed[2], 96, 1), last)
+            a_ref[h, rows, 256:384] = jnp.concatenate(mixed + [last], 0).astype(BF16)
+        return carry
+
+    lax.fori_loop(0, NZ, unpack, 0)
+    a0 = a_ref[0]
+    a1 = a_ref[1]
 
     def merid(jt, carry):
         cols = pl.ds(pl.multiple_of(jt * 256, 256), 256)
-        prod = jnp.dot(a0, tab[: 16 * LATP, cols], preferred_element_type=F32)
-        prod = prod + jnp.dot(a1, tab[16 * LATP :, cols], preferred_element_type=F32)
+        prod = jnp.dot(a0, tab[:384, cols], preferred_element_type=F32)
+        prod = prod + jnp.dot(a1, tab[384:, cols], preferred_element_type=F32)
         for l in range(NLEV):
             c0 = prod[l * 48 : l * 48 + 24]
             c1 = prod[l * 48 + 24 : l * 48 + 48]
@@ -248,6 +257,7 @@
         in_specs=[vm] * 2,
         out_specs=vm,
         scratch_shapes=[
+            pltpu.VMEM((NH, 768, 384), BF16),
             pltpu.VMEM((3, NLEV * VS, 128), F32),
             pltpu.VMEM((3, NLEV * VS, 128), F32),
         ],
@@ -268,6 +278,7 @@
         out_shape=jax.ShapeDtypeStruct((6, KL, NLEV, NL), F32),
         in_specs=[pl.BlockSpec((16, 16, NL), lambda i: (0, i, 0))],
         out_specs=pl.BlockSpec((1, KL, NLEV, NL), lambda i: (i, 0, 0, 0)),
+        compiler_params=pltpu.CompilerParams(vmem_limit_bytes=16 << 20),
         name="place",
     )(r)
 
@@ -279,7 +290,7 @@
     r = lax.all_to_all(z, ("core", "x", "y"), 0, 0, tiled=True)
     y = split_waves(r.reshape(2, 16, LATP, 768))
     r2 = lax.all_to_all(y, ("zl", "zh"), 0, 0, tiled=True)
-    c = pairs(r2.reshape(8, 2, 96, 384), merid_table())
+    c = pairs(r2.reshape(NZ, NH, SLOT, 128), merid_table())
     r3 = lax.all_to_all(c, ("zl", "core"), 0, 0, tiled=True)
     out = place(r3)
     out = out.reshape(2, NV, 1, KL, NLEV, NL)

time: 186 us -> 179 us (0.962)
  blocking collectives: 93.3 us -> 160 us
  waiting for transfers between devices: 56.7 us -> 0 us
  starting transfers between devices: 13.1 us -> 0 us
  Pallas kernels: 22.2 us -> 19.3 us
    all_to_all x0 -> x1, blocking collectives: none -> 64.9 us  [on_device(): r2 = lax.all_to_all(y, ('zl', 'zh'), 0, 0, tiled=True)]
    all_to_all x1 -> x0, waiting for transfers between devices: 56.7 us -> none  [on_device(): r2 = lax.all_to_all(y, ('zl', 'zh'), 0, 0, tiled=True)]
    all_to_all x1 -> x0, starting transfers between devices: 13.1 us -> none  [on_device(): r2 = lax.all_to_all(y, ('zl', 'zh'), 0, 0, tiled=True)]
    pallas_call x1, Pallas kernels: 4.6 us -> 2.47 us  [place(): pl.pallas_call(place_kernel, grid=(6,), out_shape=jax.ShapeDtypeStruct((6...]
    pallas_call x2 -> x1, Pallas kernels: 4.07 us -> 2.62 us  [split_waves(): pl.pallas_call(split_kernel, out_shape=jax.ShapeDtypeStruct((16, SLOT, 12...]
  transfers between devices with their start and end apart: 1 -> 0, of which waited for: 1 -> 0; matrix products, arithmetic and copies ran while one was open for 0% -> 0% of each run, Pallas kernels for 0% -> 0%
where the time goes in v3:
time: 179 us
  blocking collectives  160 us (89%)
  Pallas kernels  19.3 us (11%)
    all_to_all x1, blocking collectives, on_device(): r3 = lax.all_to_all(c, ('zl', 'core'), 0, 0, tiled=True)  65.2 us
    all_to_all x1, blocking collectives, on_device(): r2 = lax.all_to_all(y, ('zl', 'zh'), 0, 0, tiled=True)  64.9 us
    all_to_all x1, blocking collectives, on_device(): r = lax.all_to_all(z, ('core', 'x', 'y'), 0, 0, tiled=True)  29.4 us
    pallas_call x1, Pallas kernels, zonal(): pl.pallas_call(zonal_kernel, out_shape=jax.ShapeDtypeStruct((32, LATP, 76...  7.56 us
    pallas_call x1, Pallas kernels, pairs(): pl.pallas_call(pairs_kernel, out_shape=jax.ShapeDtypeStruct((NLEV, 96, NL...  6.64 us

profile of v3, /device:TPU:1, one launch (start us, length us, event | category | flops | bytes accessed | tf_op | source)
XLA Modules:
  0.0 178.9 jit_solution(8517478536200030252)
XLA Ops:
  0.0 7.6 %zonal.1 = bf16[32,24,768]{2,1,0:T(8,128)(2,1)} custom-call(bf16[66,8,1440]{2,1,0:T(8,128)(2,1)} %bitcast.19, bf16[66,8,1440]{2,1,0:T(8,128)(2,1)} %bitcast.20, f32[160,1024]{1,0:T(8,128)} %constant.4.clone.f_hbm), custom_call_target="tpu_custom_call" | custom-call | tf_op jit(solution)/shard_map/zonal/pallas_call | solution.py:127
  7.6 29.4 %all_to_all.15 = bf16[32,24,768]{2,1,0:T(8,128)(2,1)S(1)} all-to-all(bf16[32,24,768]{2,1,0:T(8,128)(2,1)} %zonal.1), channel_id=1, replica_groups=mesh['zl'=8,'core'=2,'x'=4,'zh'=2,'y'=4] {'core','x','y'}, dimensions={0} | all-to-all | bytes 2359296 | tf_op jit(solution)/shard_map/all_to_all | solution.py:290
  37.0 2.6 %split_waves.1 = bf16[16,264,128]{2,1,0:T(8,128)(2,1)S(1)} custom-call(bf16[2,16,24,768]{3,2,1,0:T(8,128)(2,1)S(1)} %bitcast.17), custom_call_target="tpu_custom_call" | custom-call | tf_op jit(solution)/shard_map/split_waves/pallas_call | solution.py:183
  39.6 0.0 copy-start
  39.6 64.9 %all_to_all.16 = bf16[16,264,128]{2,1,0:T(8,128)(2,1)S(1)} all-to-all(bf16[16,264,128]{2,1,0:T(8,128)(2,1)S(1)} %split_waves.1), channel_id=1, replica_groups=mesh['zl'=8,'core'=2,'x'=4,'zh'=2,'y'=4] {'zl','zh'}, dimensions={0} | all-to-all | bytes 2162688 | tf_op jit(solution)/shard_map/all_to_all | solution.py:292
  104.5 0.0 copy-done
  104.5 6.6 %pairs.1 = bf16[16,96,384]{2,1,0:T(8,128)(2,1)S(1)} custom-call(bf16[8,2,264,128]{3,2,1,0:T(8,128)(2,1)S(1)} %bitcast.18, bf16[768,768]{1,0:T(8,128)(2,1)S(1)} %copy-done), custom_call_target="tpu_custom_call" | custom-call | tf_op jit(solution)/shard_map/pairs/pallas_call | solution.py:254
  111.2 65.2 %all_to_all.17.r_ref = bf16[16,96,384]{2,1,0:T(8,128)(2,1)S(1)} all-to-all(bf16[16,96,384]{2,1,0:T(8,128)(2,1)S(1)} %pairs.1), channel_id=1, replica_groups=mesh['zl'=8,'core'=2,'x'=4,'zh'=2,'y'=4] {'zl','core'}, dimensions={0} | all-to-all | bytes 2359296 | tf_op jit(solution)/shard_map/all_to_all | solution.py:294
  176.4 2.5 %place.1 = f32[6,14,16,384]{3,2,1,0:T(8,128)} custom-call(bf16[16,96,384]{2,1,0:T(8,128)(2,1)S(1)} %all_to_all.17.r_ref), custom_call_target="tpu_custom_call" | custom-call | tf_op jit(solution)/shard_map/place/pallas_call | solution.py:275
Async XLA Ops:
  39.6 64.9 %copy-start = (bf16[768,768]{1,0:T(8,128)(2,1)S(1)}, bf16[768,768]{1,0:T(8,128)(2,1)}, u32[]{:S(2)}) copy-start(bf16[768,768]{1,0:T(8,128)(2,1)} %constant.8.tab) | copy-start | bytes 3538948

commit v4 on v3

--- a/solution.py
+++ b/solution.py
@@ -7,6 +7,7 @@
 from jax.experimental import pallas as pl
 from jax.experimental.pallas import tpu as pltpu
 from jax.sharding import Mesh, PartitionSpec as P
+
 
 LON, LAT, MK, NL = 1440, 704, 448, 384
 NV, NS, NLEV = 3, 8, 16
@@ -61,22 +62,29 @@
 ROWS = LATL * VS
 
 
-def zonal_kernel(fl_hbm, fs_hbm, f_hbm, out_ref, fl, fs, fac, xs, tab, zs, sem):
+def zonal_kernel(fl_hbm, fs_hbm, f_hbm, out_ref, fl, fs, fac, xs, t0, t1, t2, t3, z0, z1, z2, z3, sem):
+    tabs, zs = (t0, t1, t2, t3), (z0, z1, z2, z3)
     cp0 = pltpu.make_async_copy(f_hbm, fac, sem.at[0])
     cp1 = pltpu.make_async_copy(fl_hbm, fl, sem.at[1])
     cp2 = pltpu.make_async_copy(fs_hbm, fs, sem.at[2])
     cp0.start()
     cp1.start()
     cp2.start()
-    zs[:, ROWS:, :] = jnp.zeros((8, VS * LATP - ROWS, 128), F32)
+    for z in zs:
+        z[:, ROWS:, :] = jnp.zeros((2, VS * LATP - ROWS, 128), F32)
     cp0.wait()
 
-    def gen(i, carry):
-        row = fac[pl.ds(i, 1), :] * fac[96:128, :] + fac[pl.ds(48 + i, 1), :] * fac[128:160, :]
-        tab[pl.ds(pl.multiple_of(i * X0, X0), X0), :] = row.astype(BF16)
-        return carry
-
-    lax.fori_loop(0, X1, gen, 0)
+    def gen_rows(n, i):
+        cols = slice(n * 256, (n + 1) * 256)
+        row = fac[pl.ds(i, 1), cols] * fac[96:128, cols] + fac[pl.ds(48 + i, 1), cols] * fac[128:160, cols]
+        return row.astype(BF16)
+
+    def gen_first(i, carry):
+        for j in range(3):
+            t0[pl.ds(pl.multiple_of((i * 3 + j) * X0, X0), X0), :] = gen_rows(0, i * 3 + j)
+        return carry
+
+    lax.fori_loop(0, X1 // 3, gen_first, 0)
     cp1.wait()
     cp2.wait()
 
@@ -87,23 +95,14 @@
         return carry
 
     lax.fori_loop(0, 11, diff, 0)
-
-    def mm(n, carry):
-        w = tab[:, pl.ds(pl.multiple_of(n * 256, 256), 256)]
-        z = jnp.dot(xs[...], w, preferred_element_type=F32)
-        zs[2 * n, :ROWS, :] = z[:, :128]
-        zs[2 * n + 1, :ROWS, :] = z[:, 128:]
-        return carry
-
-    lax.fori_loop(0, 4, mm, 0)
-
     lane = lax.broadcasted_iota(jnp.int32, (LATP, 128), 1)
     hi = lane >= 64
     odd = (lane // 32) % 2 == 1
 
-    def move(d, carry):
+    def move(n, half):
+        d = 2 * n + half
         for g in range(6):
-            a = [zs[d, pl.ds(4 * g + i, LATP, stride=VS), :] for i in range(4)]
+            a = [zs[n][half, pl.ds(4 * g + i, LATP, stride=VS), :] for i in range(4)]
             b = [None] * 4
             for i in range(2):
                 b[i] = jnp.where(hi, pltpu.roll(a[i + 2], 64, 1), a[i])
@@ -114,9 +113,19 @@
                 o[j + 1] = jnp.where(odd, b[j + 1], pltpu.roll(b[j], 96, 1))
             for j in range(4):
                 out_ref[4 * d + j, :, 128 * g : 128 * (g + 1)] = o[j].astype(BF16)
-        return carry
-
-    lax.fori_loop(0, 8, move, 0)
+
+    for n in range(4):
+        z = jnp.dot(xs[...], tabs[n][...], preferred_element_type=F32)
+        if n < 3:
+            for i in range(X1):
+                tabs[n + 1][i * X0 : (i + 1) * X0, :] = gen_rows(n + 1, i)
+        if n:
+            move(n - 1, 0)
+            move(n - 1, 1)
+        zs[n][0, :ROWS, :] = z[:, :128]
+        zs[n][1, :ROWS, :] = z[:, 128:]
+    move(3, 0)
+    move(3, 1)
 
 
 def zonal(fl, fs):
@@ -134,10 +143,11 @@
             pltpu.VMEM((66, 8, LON), BF16),
             pltpu.VMEM((160, 1024), F32),
             pltpu.VMEM((ROWS, LON), BF16),
-            pltpu.VMEM((LON, 1024), BF16),
-            pltpu.VMEM((8, VS * LATP, 128), F32),
-            pltpu.SemaphoreType.DMA((3,)),
-        ],
+        ]
+        + [pltpu.VMEM((LON, 256), BF16)] * 4
+        + [pltpu.VMEM((2, VS * LATP, 128), F32)] * 4
+        + [pltpu.SemaphoreType.DMA((3,))],
+        compiler_params=pltpu.CompilerParams(vmem_limit_bytes=65_600_000),
         name="zonal",
     )(fl, fs, jnp.asarray(fac))
 
@@ -146,6 +156,7 @@
 
 
 def split_kernel(r_ref, y_ref, pack, w):
+    core = lax.axis_index("core")
     for lev in range(2):
 
         def turn(g, carry):
@@ -163,7 +174,7 @@
     tail = lax.broadcasted_iota(jnp.int32, (VS, 128), 1) >= 96
 
     def pick(kidx, carry):
-        slot = (kidx % 7) * 2 + kidx // 7
+        slot = (kidx % 7 + core) * 2 + kidx // 7
         combos = [(lev, u) for lev in range(2) for u in range(2)]
         for t in range(2):
             rows = [w[lev, t, pl.ds(kidx * 2 + u, VS, stride=32), :] for lev, u in combos]
@@ -174,8 +185,8 @@
         return carry
 
     lax.fori_loop(0, 14, pick, 0)
-    y_ref[14, :, :] = jnp.zeros((SLOT, 128), BF16)
-    y_ref[15, :, :] = jnp.zeros((SLOT, 128), BF16)
+    for h in range(NH):
+        y_ref[14 * (1 - core) + h, :, :] = jnp.zeros((SLOT, 128), BF16)
 
 
 def split_waves(r):
@@ -191,7 +202,37 @@
     )(r)
 
 
-def pairs_kernel(r_ref, tab, out_ref, a_ref, sre, sim):
+def products(sre, sim, outs, first):
+    zl, core = lax.axis_index("zl"), lax.axis_index("core")
+
+    def block(n, carry):
+        jt = n // NV
+        v = n % NV
+        bre = [sre[jt, pl.ds(v * NS + s, NLEV, stride=VS), :] for s in range(NS)]
+        bim = [sim[jt, pl.ds(v * NS + s, NLEV, stride=VS), :] for s in range(NS)]
+        lanes = pl.ds(pl.multiple_of(jt * 128, 128), 128)
+        for i, out_ref in enumerate(outs):
+
+            def one(half, inner):
+                base = ((zl ^ (first + i)) * 2 + (core ^ half)) * VS + v * NS
+                co = jnp.zeros((NLEV, 128), F32)
+                qd = jnp.zeros((NLEV, 128), F32)
+                for s in range(NS):
+                    ar = sre[jt, pl.ds(base + s, NLEV, stride=0), :]
+                    ai = sim[jt, pl.ds(base + s, NLEV, stride=0), :]
+                    co = co + ar * bre[s] + ai * bim[s]
+                    qd = qd + ai * bre[s] - ar * bim[s]
+                out_ref[half, pl.ds(pl.multiple_of(v * 16, 16), 16), lanes] = (co * (1.0 / NS)).astype(BF16)
+                out_ref[half, pl.ds(pl.multiple_of(48 + v * 16, 16), 16), lanes] = (qd * (1.0 / NS)).astype(BF16)
+                return inner
+
+            lax.fori_loop(0, 2, one, 0)
+        return carry
+
+    lax.fori_loop(0, 3 * NV, block, 0)
+
+
+def far_kernel(r_ref, tab, sre, sim, o4, o5, o6, o7, a_ref):
     tail = lax.broadcasted_iota(jnp.int32, (VS, 128), 1)
 
     def unpack(z, carry):
@@ -223,64 +264,92 @@
 
     lax.fori_loop(0, 3, merid, 0)
 
-    def block(n, carry):
-        jt = n // NV
-        v = n % NV
-        bre = [sre[jt, pl.ds(v * NS + s, NLEV, stride=VS), :] for s in range(NS)]
-        bim = [sim[jt, pl.ds(v * NS + s, NLEV, stride=VS), :] for s in range(NS)]
-
-        def one(a, inner):
-            base = a * VS + v * NS
-            co = jnp.zeros((NLEV, 128), F32)
-            qd = jnp.zeros((NLEV, 128), F32)
-            for s in range(NS):
-                ar = sre[jt, pl.ds(base + s, NLEV, stride=0), :]
-                ai = sim[jt, pl.ds(base + s, NLEV, stride=0), :]
-                co = co + ar * bre[s] + ai * bim[s]
-                qd = qd + ai * bre[s] - ar * bim[s]
-            lanes = pl.ds(pl.multiple_of(jt * 128, 128), 128)
-            out_ref[a, pl.ds(pl.multiple_of(v * 16, 16), 16), lanes] = (co * (1.0 / NS)).astype(BF16)
-            out_ref[a, pl.ds(pl.multiple_of(48 + v * 16, 16), 16), lanes] = (qd * (1.0 / NS)).astype(BF16)
-            return inner
-
-        lax.fori_loop(0, NLEV, one, 0)
-        return carry
-
-    lax.fori_loop(0, 3 * NV, block, 0)
-
-
-def pairs(r, tab):
+    products(sre, sim, (o4, o5, o6, o7), 4)
+
+
+def near_kernel(sre, sim, o0, o1, o2, o3):
+    products(sre, sim, (o0, o1, o2, o3), 0)
+
+
+ROWSET = jax.ShapeDtypeStruct((2, 96, NL), BF16)
+SPEC = jax.ShapeDtypeStruct((3, NLEV * VS, 128), F32)
+
+
+def far_pairs(r, tab):
     vm = pl.BlockSpec(memory_space=pltpu.VMEM)
     return pl.pallas_call(
-        pairs_kernel,
-        out_shape=jax.ShapeDtypeStruct((NLEV, 96, NL), BF16),
-        in_specs=[vm] * 2,
-        out_specs=vm,
-        scratch_shapes=[
-            pltpu.VMEM((NH, 768, 384), BF16),
-            pltpu.VMEM((3, NLEV * VS, 128), F32),
-            pltpu.VMEM((3, NLEV * VS, 128), F32),
-        ],
-        compiler_params=pltpu.CompilerParams(vmem_limit_bytes=40 << 20),
-        name="pairs",
+        far_kernel,
+        out_shape=[SPEC] * 2 + [ROWSET] * 4,
+        in_specs=[vm, vm],
+        out_specs=[vm] * 6,
+        scratch_shapes=[pltpu.VMEM((NH, 768, 384), BF16)],
+        compiler_params=pltpu.CompilerParams(vmem_limit_bytes=24 << 20),
+        name="far_pairs",
     )(r, tab)
 
 
-def place_kernel(r_ref, out_ref):
-    for k in range(KL):
-        out_ref[0, k] = r_ref[k].astype(F32)
-
-
-def place(r):
-    return pl.pallas_call(
-        place_kernel,
-        grid=(6,),
+def near_pairs(sre, sim):
+    vm = pl.BlockSpec(memory_space=pltpu.VMEM)
+    return pl.pallas_call(
+        near_kernel,
+        out_shape=[ROWSET] * 4,
+        in_specs=[vm, vm],
+        out_specs=[vm] * 4,
+        cost_estimate=pl.CostEstimate(flops=3_000_000_000, bytes_accessed=1_800_000, transcendentals=0),
+        compiler_params=pltpu.CompilerParams(vmem_limit_bytes=16 << 20),
+        name="near_pairs",
+    )(sre, sim)
+
+
+def place_kernel(chips, keep, *refs):
+    n = 2 * len(chips)
+    blocks, out, bufs, sem = refs[:n], refs[n + keep], refs[n + keep + 1], refs[n + keep + 2]
+    zl, core = lax.axis_index("zl"), lax.axis_index("core")
+    source = [((zl ^ d) - (core ^ half), core ^ half) for half in range(2) for d in chips]
+
+    def copy(i):
+        step, parity = source[i]
+        return pltpu.make_async_copy(bufs.at[i], out.at[:, 2 * step + parity], sem.at[i])
+
+    for i in range(n):
+
+        @pl.when((source[i][0] >= 0) & (source[i][0] <= 6))
+        def _():
+            for cv in range(6):
+                bufs[i, cv] = blocks[i][0, cv * 16 : (cv + 1) * 16, :].astype(F32)
+            copy(i).start()
+
+    for i in range(n):
+
+        @pl.when((source[i][0] >= 0) & (source[i][0] <= 6))
+        def _():
+            copy(i).wait()
+
+
+def place(chips, blocks, out=None):
+    n, keep = len(blocks), int(out is not None)
+    specs = [pl.BlockSpec((1, 96, NL), lambda i, j=j: (j, 0, 0)) for _, j in blocks]
+    return pl.pallas_call(
+        lambda *refs: place_kernel(chips, keep, *refs),
+        grid=(1,),
         out_shape=jax.ShapeDtypeStruct((6, KL, NLEV, NL), F32),
-        in_specs=[pl.BlockSpec((16, 16, NL), lambda i: (0, i, 0))],
-        out_specs=pl.BlockSpec((1, KL, NLEV, NL), lambda i: (i, 0, 0, 0)),
-        compiler_params=pltpu.CompilerParams(vmem_limit_bytes=16 << 20),
-        name="place",
-    )(r)
+        in_specs=specs + [pl.BlockSpec(memory_space=pl.ANY)] * keep,
+        out_specs=pl.BlockSpec(memory_space=pl.ANY),
+        scratch_shapes=[pltpu.VMEM((n, 6, NLEV, NL), F32), pltpu.SemaphoreType.DMA((n,))],
+        input_output_aliases={n: 0} if keep else {},
+        cost_estimate=pl.CostEstimate(flops=1_000_000, bytes_accessed=220_000 * n, transcendentals=0),
+        compiler_params=pltpu.CompilerParams(vmem_limit_bytes=24 << 20),
+        name="place_rest" if keep else "place_first",
+    )(*[a for a, _ in blocks], *([out] if keep else []))
+
+
+def toward(block, d):
+    route = [(z * NC + c, (z ^ d) * NC + c) for z in range(NZ) for c in range(NC) if 0 <= z - c <= 6]
+    return lax.ppermute(block, ("zl", "core"), route)
+
+
+def swap_cores(blocks):
+    return lax.ppermute(jnp.stack(blocks), "core", [(0, 1), (1, 0)])
 
 
 def on_device(fc_long, fc_short):
@@ -290,9 +359,20 @@
     r = lax.all_to_all(z, ("core", "x", "y"), 0, 0, tiled=True)
     y = split_waves(r.reshape(2, 16, LATP, 768))
     r2 = lax.all_to_all(y, ("zl", "zh"), 0, 0, tiled=True)
-    c = pairs(r2.reshape(NZ, NH, SLOT, 128), merid_table())
-    r3 = lax.all_to_all(c, ("zl", "core"), 0, 0, tiled=True)
-    out = place(r3)
+    sre, sim, *far = far_pairs(r2.reshape(NZ, NH, SLOT, 128), merid_table())
+    got = {}
+    for d in (4, 5, 6, 7):
+        got[d] = toward(far[d - 4], d)
+    near = near_pairs(sre, sim)
+    got[0] = near[0]
+    for d in (3, 2, 1):
+        got[d] = toward(near[d], d)
+    early, late = (0, 1, 2, 3, 4, 5), (6, 7)
+    out = None
+    for group in (early, late):
+        swapped = swap_cores([got[d][1] for d in group])
+        blocks = [(got[d], 0) for d in group] + [(swapped, i) for i in range(len(group))]
+        out = place(group, blocks, out)
     out = out.reshape(2, NV, 1, KL, NLEV, NL)
     return jnp.swapaxes(out, 3, 4)
 

time: 179 us -> 179 us (level)
  the two profiles are of different devices: /device:TPU:1 before, /device:TPU:97 now
where the time goes in v4:
time: 179 us; the launch traced here: 178 us
  blocking collectives  89 us (50%)
  waiting for transfers between devices  35.8 us (20%)
  starting transfers between devices  35.3 us (20%)
  Pallas kernels  18.1 us (10%)
    all_to_all x1, blocking collectives, on_device(): r2 = lax.all_to_all(y, ('zl', 'zh'), 0, 0, tiled=True)  62.4 us
    ppermute x7, waiting for transfers between devices, toward(): return lax.ppermute(block, ('zl', 'core'), route)  35.7 us
    ppermute x7, starting transfers between devices, toward(): return lax.ppermute(block, ('zl', 'core'), route)  27.5 us
    all_to_all x1, blocking collectives, on_device(): r = lax.all_to_all(z, ('core', 'x', 'y'), 0, 0, tiled=True)  26.6 us
    ppermute x2, starting transfers between devices, swap_cores(): return lax.ppermute(jnp.stack(blocks), 'core', [(0, 1), (1, 0)])  7.78 us
    pallas_call x1, Pallas kernels, zonal(): pl.pallas_call(zonal_kernel, out_shape=jax.ShapeDtypeStruct((32, LATP, 76...  6.09 us
    pallas_call x1, Pallas kernels, far_pairs(): pl.pallas_call(far_kernel, out_shape=[SPEC] * 2 + [ROWSET] * 4, in_specs=...  4.95 us
  transfers between devices with their start and end apart: 9, of which 4 were waited for; matrix products, arithmetic and copies ran while one was open for 0% of the time, Pallas kernels for 2%

profile of v4, /device:TPU:97, one launch (start us, length us, event | category | flops | bytes accessed | tf_op | source)
XLA Modules:
  0.0 178.5 jit_solution(4762753950873432843)
XLA Ops:
  0.0 6.1 %zonal.1 = bf16[32,24,768]{2,1,0:T(8,128)(2,1)} custom-call(bf16[66,8,1440]{2,1,0:T(8,128)(2,1)} %bitcast.19, bf16[66,8,1440]{2,1,0:T(8,128)(2,1)} %bitcast.20, f32[160,1024]{1,0:T(8,128)} %constant.4.clone.f_hbm), custom_call_target="tpu_custom_call" | custom-call | tf_op jit(solution)/shard_map/zonal/pallas_call | solution.py:136
  6.1 26.6 %all_to_all.10 = bf16[32,24,768]{2,1,0:T(8,128)(2,1)S(1)} all-to-all(bf16[32,24,768]{2,1,0:T(8,128)(2,1)} %zonal.1), channel_id=1, replica_groups=mesh['zl'=8,'core'=2,'x'=4,'zh'=2,'y'=4] {'core','x','y'}, dimensions={0} | all-to-all | bytes 2359296 | tf_op jit(solution)/shard_map/all_to_all | solution.py:359
  32.7 2.6 %split_waves.1 = bf16[16,264,128]{2,1,0:T(8,128)(2,1)S(1)} custom-call(bf16[2,16,24,768]{3,2,1,0:T(8,128)(2,1)S(1)} %bitcast.17), custom_call_target="tpu_custom_call" | custom-call | tf_op jit(solution)/shard_map/split_waves/pallas_call | solution.py:194
  35.3 0.0 copy-start
  35.3 62.4 %all_to_all.11 = bf16[16,264,128]{2,1,0:T(8,128)(2,1)S(1)} all-to-all(bf16[16,264,128]{2,1,0:T(8,128)(2,1)S(1)} %split_waves.1), channel_id=1, replica_groups=mesh['zl'=8,'core'=2,'x'=4,'zh'=2,'y'=4] {'zl','zh'}, dimensions={0} | all-to-all | bytes 2162688 | tf_op jit(solution)/shard_map/all_to_all | solution.py:361
  97.7 0.0 copy-done
  97.7 5.0 %far_pairs.1 = (f32[3,384,128]{2,1,0:T(8,128)S(1)}, f32[3,384,128]{2,1,0:T(8,128)S(1)}, bf16[2,96,384]{2,1,0:T(8,128)(2,1)S(1)}, bf16[2,96,384]{2,1,0:T(8,128)(2...) custom-call(bf16[8,2,264,128]{3,2,1,0:T(8,128)(2,1)S(1)} %bitcast.18, bf16[768,768]{1,0:T(8,128)(2,1)S(1)} %copy-done), custom_call_target="tpu_custom_call" | custom-call | tf_op jit(solution)/shard_map/far_pairs/pallas_call | solution.py:280
  102.7 7.9 %collective-permute-start.6 = (bf16[2,96,384]{2,1,0:T(8,128)(2,1)S(1)}, bf16[2,96,384]{2,1,0:T(8,128)(2,1)S(1)}, u32[]{:S(2)}, u32[]{:S(2)}) collective-permute-start(bf16[2,96,384]{2,1,0:T(8,128)(2,1)S(1)} %get-tuple-element.23), channel_id=1, source_target_pairs={{0,256},{64,320},{96,352},{128,384},{160,416},{192,448},{224,480},... | collective-permute-start | bytes 442376 | tf_op jit(solution)/shard_map/ppermute | solution.py:348
  110.6 1.9 %collective-permute-start.7 = (bf16[2,96,384]{2,1,0:T(8,128)(2,1)S(1)}, bf16[2,96,384]{2,1,0:T(8,128)(2,1)S(1)}, u32[]{:S(2)}, u32[]{:S(2)}) collective-permute-start(bf16[2,96,384]{2,1,0:T(8,128)(2,1)S(1)} %get-tuple-element.24), channel_id=1, source_target_pairs={{0,320},{64,256},{96,288},{128,448},{160,480},{192,384},{224,416},... | collective-permute-start | bytes 442376 | tf_op jit(solution)/shard_map/ppermute | solution.py:348
  112.5 2.4 %near_pairs.1 = (bf16[2,96,384]{2,1,0:T(8,128)(2,1)S(1)}, bf16[2,96,384]{2,1,0:T(8,128)(2,1)S(1)}, bf16[2,96,384]{2,1,0:T(8,128)(2,1)S(1)}, bf16[2,96,384]{2,1,0:T(8,128)(2,1)S(1)}) custom-call(f32[3,384,128]{2,1,0:T(8,128)S(1)} %get-tuple-element.17.sre, f32[3,384,128]{2,1,0:T(8,128)S(1)} %get-tuple-element.18.sim), custom_call_target="tpu_custom_call" | custom-call | flops 3000000000 | bytes 1800000 | tf_op jit(solution)/shard_map/near_pairs/pallas_call | solution.py:293
  114.9 3.1 %collective-permute-start.3 = (bf16[2,96,384]{2,1,0:T(8,128)(2,1)S(1)}, bf16[2,96,384]{2,1,0:T(8,128)(2,1)S(1)}, u32[]{:S(2)}, u32[]{:S(2)}) collective-permute-start(bf16[2,96,384]{2,1,0:T(8,128)(2,1)S(1)} %get-tuple-element.20), channel_id=1, source_target_pairs={{0,64},{64,0},{96,32},{128,192},{160,224},{192,128},{224,160},{256... | collective-permute-start | bytes 442376 | tf_op jit(solution)/shard_map/ppermute | solution.py:348
  118.0 2.3 %collective-permute-start.4 = (bf16[2,96,384]{2,1,0:T(8,128)(2,1)S(1)}, bf16[2,96,384]{2,1,0:T(8,128)(2,1)S(1)}, u32[]{:S(2)}, u32[]{:S(2)}) collective-permute-start(bf16[2,96,384]{2,1,0:T(8,128)(2,1)S(1)} %get-tuple-element.21), channel_id=1, source_target_pairs={{0,128},{64,192},{96,224},{128,0},{160,32},{192,64},{224,96},{256,... | collective-permute-start | bytes 442376 | tf_op jit(solution)/shard_map/ppermute | solution.py:348
  120.3 1.3 collective-permute-start.5
  121.6 12.2 %collective-permute-done.3.refs_1_ = bf16[2,96,384]{2,1,0:T(8,128)(2,1)S(1)} collective-permute-done((bf16[2,96,384]{2,1,0:T(8,128)(2,1)S(1)}, bf16[2,96,384]{2,1,0:T(8,128)(2,1)S(1)}, u32[]{:S(2)}, u32[]{:S(2)}) %collective-permute-start.3) | collective-permute-done | bytes 147488 | tf_op jit(solution)/shard_map/ppermute | solution.py:348
  133.9 0.0 collective-permute-done.4.refs_2_
  133.9 3.0 %collective-permute-done.5.refs_3_ = bf16[2,96,384]{2,1,0:T(8,128)(2,1)S(1)} collective-permute-done((bf16[2,96,384]{2,1,0:T(8,128)(2,1)S(1)}, bf16[2,96,384]{2,1,0:T(8,128)(2,1)S(1)}, u32[]{:S(2)}, u32[]{:S(2)}) %collective-permute-start.5) | collective-permute-done | bytes 147488 | tf_op jit(solution)/shard_map/ppermute | solution.py:348
  137.0 0.0 collective-permute-done.6.refs_4_
  137.0 0.0 collective-permute-done.7.refs_5_
  137.0 5.0 %collective-permute-start.8 = (bf16[6,96,384]{2,1,0:T(8,128)(2,1)S(1)}, bf16[6,96,384]{2,1,0:T(8,128)(2,1)S(1)}, u32[]{:S(2)}, u32[]{:S(2)}) collective-permute-start(bf16[6,96,384]{2,1,0:T(8,128)(2,1)S(1)} %slice_dynamic-update-slice_fusion), channel_id=1, source_target_pairs={{0,32},{32,0},{1,33},{33,1},{2,34},{34,2},{3,35},{35,3},{4,36},{36... | collective-permute-start | bytes 1327112 | tf_op jit(solution)/shard_map/ppermute | solution.py:352
  142.0 9.1 %collective-permute-start = (bf16[2,96,384]{2,1,0:T(8,128)(2,1)S(1)}, bf16[2,96,384]{2,1,0:T(8,128)(2,1)S(1)}, u32[]{:S(2)}, u32[]{:S(2)}) collective-permute-start(bf16[2,96,384]{2,1,0:T(8,128)(2,1)S(1)} %get-tuple-element.15), channel_id=1, source_target_pairs={{0,384},{64,448},{96,480},{128,256},{160,288},{192,320},{224,352},... | collective-permute-start | bytes 442376 | tf_op jit(solution)/shard_map/ppermute | solution.py:348
  151.1 1.9 %collective-permute-start.1 = (bf16[2,96,384]{2,1,0:T(8,128)(2,1)S(1)}, bf16[2,96,384]{2,1,0:T(8,128)(2,1)S(1)}, u32[]{:S(2)}, u32[]{:S(2)}) collective-permute-start(bf16[2,96,384]{2,1,0:T(8,128)(2,1)S(1)} %get-tuple-element.16), channel_id=1, source_target_pairs={{0,448},{64,384},{96,416},{128,320},{160,352},{192,256},{224,288},... | collective-permute-start | bytes 442376 | tf_op jit(solution)/shard_map/ppermute | solution.py:348
  153.1 15.0 %collective-permute-done.refs_0_ = bf16[2,96,384]{2,1,0:T(8,128)(2,1)S(1)} collective-permute-done((bf16[2,96,384]{2,1,0:T(8,128)(2,1)S(1)}, bf16[2,96,384]{2,1,0:T(8,128)(2,1)S(1)}, u32[]{:S(2)}, u32[]{:S(2)}) %collective-permute-start) | collective-permute-done | bytes 147488 | tf_op jit(solution)/shard_map/ppermute | solution.py:348
  168.1 5.4 %collective-permute-done.1.refs_1_ = bf16[2,96,384]{2,1,0:T(8,128)(2,1)S(1)} collective-permute-done((bf16[2,96,384]{2,1,0:T(8,128)(2,1)S(1)}, bf16[2,96,384]{2,1,0:T(8,128)(2,1)S(1)}, u32[]{:S(2)}, u32[]{:S(2)}) %collective-permute-start.1) | collective-permute-done | bytes 147488 | tf_op jit(solution)/shard_map/ppermute | solution.py:348
  173.6 2.8 %collective-permute-start.2 = (bf16[2,96,384]{2,1,0:T(8,128)(2,1)S(1)}, bf16[2,96,384]{2,1,0:T(8,128)(2,1)S(1)}, u32[]{:S(2)}, u32[]{:S(2)}) collective-permute-start(bf16[2,96,384]{2,1,0:T(8,128)(2,1)S(1)} %pad_maximum_fusion), channel_id=1, source_target_pairs={{0,32},{32,0},{1,33},{33,1},{2,34},{34,2},{3,35},{35,3},{4,36},{36... | collective-permute-start | bytes 442376 | tf_op jit(solution)/shard_map/ppermute | solution.py:352
  176.3 0.0 collective-permute-done.8.refs_6_.refs_7_.refs_8_.refs_9_.refs_10_.refs_11_
  176.4 1.2 place_first.1.refs_4_
  177.6 0.0 collective-permute-done.2.refs_2_.refs_3_
  177.6 0.9 place_rest.1
  (9 shorter events, 0.1 us)
Async XLA Ops:
  35.3 62.4 %copy-start = (bf16[768,768]{1,0:T(8,128)(2,1)S(1)}, bf16[768,768]{1,0:T(8,128)(2,1)}, u32[]{:S(2)}) copy-start(bf16[768,768]{1,0:T(8,128)(2,1)} %constant.8.tab) | copy-start | bytes 3538948
  102.7 34.3 %collective-permute-start.6 = (bf16[2,96,384]{2,1,0:T(8,128)(2,1)S(1)}, bf16[2,96,384]{2,1,0:T(8,128)(2,1)S(1)}, u32[]{:S(2)}, u32[]{:S(2)}) collective-permute-start(bf16[2,96,384]{2,1,0:T(8,128)(2,1)S(1)} %get-tuple-element.23), channel_id=1, source_target_pairs={{0,256},{64,320},{96,352},{128,384},{160,416},{192,448},{224,480},... | collective-permute-start | bytes 442376 | tf_op jit(solution)/shard_map/ppermute | solution.py:348
  110.6 26.4 %collective-permute-start.7 = (bf16[2,96,384]{2,1,0:T(8,128)(2,1)S(1)}, bf16[2,96,384]{2,1,0:T(8,128)(2,1)S(1)}, u32[]{:S(2)}, u32[]{:S(2)}) collective-permute-start(bf16[2,96,384]{2,1,0:T(8,128)(2,1)S(1)} %get-tuple-element.24), channel_id=1, source_target_pairs={{0,320},{64,256},{96,288},{128,448},{160,480},{192,384},{224,416},... | collective-permute-start | bytes 442376 | tf_op jit(solution)/shard_map/ppermute | solution.py:348
  114.9 19.0 %collective-permute-start.3 = (bf16[2,96,384]{2,1,0:T(8,128)(2,1)S(1)}, bf16[2,96,384]{2,1,0:T(8,128)(2,1)S(1)}, u32[]{:S(2)}, u32[]{:S(2)}) collective-permute-start(bf16[2,96,384]{2,1,0:T(8,128)(2,1)S(1)} %get-tuple-element.20), channel_id=1, source_target_pairs={{0,64},{64,0},{96,32},{128,192},{160,224},{192,128},{224,160},{256... | collective-permute-start | bytes 442376 | tf_op jit(solution)/shard_map/ppermute | solution.py:348
  118.0 15.9 %collective-permute-start.4 = (bf16[2,96,384]{2,1,0:T(8,128)(2,1)S(1)}, bf16[2,96,384]{2,1,0:T(8,128)(2,1)S(1)}, u32[]{:S(2)}, u32[]{:S(2)}) collective-permute-start(bf16[2,96,384]{2,1,0:T(8,128)(2,1)S(1)} %get-tuple-element.21), channel_id=1, source_target_pairs={{0,128},{64,192},{96,224},{128,0},{160,32},{192,64},{224,96},{256,... | collective-permute-start | bytes 442376 | tf_op jit(solution)/shard_map/ppermute | solution.py:348
  120.3 16.7 %collective-permute-start.5 = (bf16[2,96,384]{2,1,0:T(8,128)(2,1)S(1)}, bf16[2,96,384]{2,1,0:T(8,128)(2,1)S(1)}, u32[]{:S(2)}, u32[]{:S(2)}) collective-permute-start(bf16[2,96,384]{2,1,0:T(8,128)(2,1)S(1)} %get-tuple-element.22), channel_id=1, source_target_pairs={{0,192},{64,128},{96,160},{128,64},{160,96},{192,0},{224,32},{256,... | collective-permute-start | bytes 442376 | tf_op jit(solution)/shard_map/ppermute | solution.py:348
  137.0 39.3 %collective-permute-start.8 = (bf16[6,96,384]{2,1,0:T(8,128)(2,1)S(1)}, bf16[6,96,384]{2,1,0:T(8,128)(2,1)S(1)}, u32[]{:S(2)}, u32[]{:S(2)}) collective-permute-start(bf16[6,96,384]{2,1,0:T(8,128)(2,1)S(1)} %slice_dynamic-update-slice_fusion), channel_id=1, source_target_pairs={{0,32},{32,0},{1,33},{33,1},{2,34},{34,2},{3,35},{35,3},{4,36},{36... | collective-permute-start | bytes 1327112 | tf_op jit(solution)/shard_map/ppermute | solution.py:352
  142.0 26.0 %collective-permute-start = (bf16[2,96,384]{2,1,0:T(8,128)(2,1)S(1)}, bf16[2,96,384]{2,1,0:T(8,128)(2,1)S(1)}, u32[]{:S(2)}, u32[]{:S(2)}) collective-permute-start(bf16[2,96,384]{2,1,0:T(8,128)(2,1)S(1)} %get-tuple-element.15), channel_id=1, source_target_pairs={{0,384},{64,448},{96,480},{128,256},{160,288},{192,320},{224,352},... | collective-permute-start | bytes 442376 | tf_op jit(solution)/shard_map/ppermute | solution.py:348
  151.1 22.4 %collective-permute-start.1 = (bf16[2,96,384]{2,1,0:T(8,128)(2,1)S(1)}, bf16[2,96,384]{2,1,0:T(8,128)(2,1)S(1)}, u32[]{:S(2)}, u32[]{:S(2)}) collective-permute-start(bf16[2,96,384]{2,1,0:T(8,128)(2,1)S(1)} %get-tuple-element.16), channel_id=1, source_target_pairs={{0,448},{64,384},{96,416},{128,320},{160,352},{192,256},{224,288},... | collective-permute-start | bytes 442376 | tf_op jit(solution)/shard_map/ppermute | solution.py:348
  173.6 4.0 %collective-permute-start.2 = (bf16[2,96,384]{2,1,0:T(8,128)(2,1)S(1)}, bf16[2,96,384]{2,1,0:T(8,128)(2,1)S(1)}, u32[]{:S(2)}, u32[]{:S(2)}) collective-permute-start(bf16[2,96,384]{2,1,0:T(8,128)(2,1)S(1)} %pad_maximum_fusion), channel_id=1, source_target_pairs={{0,32},{32,0},{1,33},{33,1},{2,34},{34,2},{3,35},{35,3},{4,36},{36... | collective-permute-start | bytes 442376 | tf_op jit(solution)/shard_map/ppermute | solution.py:352

commit v5 on v4

--- a/solution.py
+++ b/solution.py
@@ -173,8 +173,9 @@
         lax.fori_loop(0, 6, turn, 0)
     tail = lax.broadcasted_iota(jnp.int32, (VS, 128), 1) >= 96
 
-    def pick(kidx, carry):
-        slot = (kidx % 7 + core) * 2 + kidx // 7
+    def pick(slot, carry):
+        zl, h = slot // 2, slot % 2
+        kidx = h * 7 + (zl + 7 - core) % 7
         combos = [(lev, u) for lev in range(2) for u in range(2)]
         for t in range(2):
             rows = [w[lev, t, pl.ds(kidx * 2 + u, VS, stride=32), :] for lev, u in combos]
@@ -184,9 +185,7 @@
         y_ref[slot, 192:SLOT, :] = jnp.concatenate(mixed, 0).astype(BF16)
         return carry
 
-    lax.fori_loop(0, 14, pick, 0)
-    for h in range(NH):
-        y_ref[14 * (1 - core) + h, :, :] = jnp.zeros((SLOT, 128), BF16)
+    lax.fori_loop(0, 16, pick, 0)
 
 
 def split_waves(r):
@@ -212,27 +211,23 @@
         bim = [sim[jt, pl.ds(v * NS + s, NLEV, stride=VS), :] for s in range(NS)]
         lanes = pl.ds(pl.multiple_of(jt * 128, 128), 128)
         for i, out_ref in enumerate(outs):
-
-            def one(half, inner):
-                base = ((zl ^ (first + i)) * 2 + (core ^ half)) * VS + v * NS
-                co = jnp.zeros((NLEV, 128), F32)
-                qd = jnp.zeros((NLEV, 128), F32)
-                for s in range(NS):
-                    ar = sre[jt, pl.ds(base + s, NLEV, stride=0), :]
-                    ai = sim[jt, pl.ds(base + s, NLEV, stride=0), :]
-                    co = co + ar * bre[s] + ai * bim[s]
-                    qd = qd + ai * bre[s] - ar * bim[s]
-                out_ref[half, pl.ds(pl.multiple_of(v * 16, 16), 16), lanes] = (co * (1.0 / NS)).astype(BF16)
-                out_ref[half, pl.ds(pl.multiple_of(48 + v * 16, 16), 16), lanes] = (qd * (1.0 / NS)).astype(BF16)
-                return inner
-
-            lax.fori_loop(0, 2, one, 0)
+            base = ((zl ^ (first + i // 2)) * 2 + (core ^ (i % 2))) * VS + v * NS
+            co = jnp.zeros((NLEV, 128), F32)
+            qd = jnp.zeros((NLEV, 128), F32)
+            for s in range(NS):
+                ar = sre[jt, pl.ds(base + s, NLEV, stride=0), :]
+                ai = sim[jt, pl.ds(base + s, NLEV, stride=0), :]
+                co = co + ar * bre[s] + ai * bim[s]
+                qd = qd + ai * bre[s] - ar * bim[s]
+            out_ref[pl.ds(pl.multiple_of(v * 16, 16), 16), lanes] = (co * (1.0 / NS)).astype(BF16)
+            out_ref[pl.ds(pl.multiple_of(48 + v * 16, 16), 16), lanes] = (qd * (1.0 / NS)).astype(BF16)
         return carry
 
     lax.fori_loop(0, 3 * NV, block, 0)
 
 
-def far_kernel(r_ref, tab, sre, sim, o4, o5, o6, o7, a_ref):
+def far_kernel(r_ref, tab, sre, sim, *refs):
+    outs, a_ref = refs[:8], refs[8]
     tail = lax.broadcasted_iota(jnp.int32, (VS, 128), 1)
 
     def unpack(z, carry):
@@ -264,14 +259,14 @@
 
     lax.fori_loop(0, 3, merid, 0)
 
-    products(sre, sim, (o4, o5, o6, o7), 4)
-
-
-def near_kernel(sre, sim, o0, o1, o2, o3):
-    products(sre, sim, (o0, o1, o2, o3), 0)
-
-
-ROWSET = jax.ShapeDtypeStruct((2, 96, NL), BF16)
+    products(sre, sim, outs, 4)
+
+
+def near_kernel(sre, sim, *outs):
+    products(sre, sim, outs, 0)
+
+
+ROWSET = jax.ShapeDtypeStruct((96, NL), BF16)
 SPEC = jax.ShapeDtypeStruct((3, NLEV * VS, 128), F32)
 
 
@@ -279,9 +274,9 @@
     vm = pl.BlockSpec(memory_space=pltpu.VMEM)
     return pl.pallas_call(
         far_kernel,
-        out_shape=[SPEC] * 2 + [ROWSET] * 4,
+        out_shape=[SPEC] * 2 + [ROWSET] * 8,
         in_specs=[vm, vm],
-        out_specs=[vm] * 6,
+        out_specs=[vm] * 10,
         scratch_shapes=[pltpu.VMEM((NH, 768, 384), BF16)],
         compiler_params=pltpu.CompilerParams(vmem_limit_bytes=24 << 20),
         name="far_pairs",
@@ -292,64 +287,65 @@
     vm = pl.BlockSpec(memory_space=pltpu.VMEM)
     return pl.pallas_call(
         near_kernel,
-        out_shape=[ROWSET] * 4,
+        out_shape=[ROWSET] * 8,
         in_specs=[vm, vm],
-        out_specs=[vm] * 4,
+        out_specs=[vm] * 8,
         cost_estimate=pl.CostEstimate(flops=3_000_000_000, bytes_accessed=1_800_000, transcendentals=0),
         compiler_params=pltpu.CompilerParams(vmem_limit_bytes=16 << 20),
         name="near_pairs",
     )(sre, sim)
 
 
-def place_kernel(chips, keep, *refs):
-    n = 2 * len(chips)
-    blocks, out, bufs, sem = refs[:n], refs[n + keep], refs[n + keep + 1], refs[n + keep + 2]
+def place_kernel(blocks, keep, *refs):
+    n = len(blocks)
+    rows, out, bufs, sem = refs[:n], refs[n + keep], refs[n + keep + 1], refs[n + keep + 2]
     zl, core = lax.axis_index("zl"), lax.axis_index("core")
-    source = [((zl ^ d) - (core ^ half), core ^ half) for half in range(2) for d in chips]
+
+    def when_sent(d):
+        return (lambda f: f()) if d < 4 else pl.when(((zl ^ d) >= 1) & ((zl ^ d) <= 6))
 
     def copy(i):
-        step, parity = source[i]
-        return pltpu.make_async_copy(bufs.at[i], out.at[:, 2 * step + parity], sem.at[i])
+        d, half = blocks[i]
+        parity = core ^ half
+        wave = 2 * (((zl ^ d) + 7 - parity) % 7) + parity
+        return pltpu.make_async_copy(bufs.at[i], out.at[:, wave], sem.at[i])
 
     for i in range(n):
 
-        @pl.when((source[i][0] >= 0) & (source[i][0] <= 6))
+        @when_sent(blocks[i][0])
         def _():
             for cv in range(6):
-                bufs[i, cv] = blocks[i][0, cv * 16 : (cv + 1) * 16, :].astype(F32)
+                bufs[i, cv] = rows[i][cv * 16 : (cv + 1) * 16, :].astype(F32)
             copy(i).start()
 
     for i in range(n):
 
-        @pl.when((source[i][0] >= 0) & (source[i][0] <= 6))
+        @when_sent(blocks[i][0])
         def _():
             copy(i).wait()
 
 
-def place(chips, blocks, out=None):
+def place(blocks, rows, out=None):
     n, keep = len(blocks), int(out is not None)
-    specs = [pl.BlockSpec((1, 96, NL), lambda i, j=j: (j, 0, 0)) for _, j in blocks]
-    return pl.pallas_call(
-        lambda *refs: place_kernel(chips, keep, *refs),
-        grid=(1,),
+    return pl.pallas_call(
+        lambda *refs: place_kernel(blocks, keep, *refs),
         out_shape=jax.ShapeDtypeStruct((6, KL, NLEV, NL), F32),
-        in_specs=specs + [pl.BlockSpec(memory_space=pl.ANY)] * keep,
+        in_specs=[pl.BlockSpec(memory_space=pltpu.VMEM)] * n + [pl.BlockSpec(memory_space=pl.ANY)] * keep,
         out_specs=pl.BlockSpec(memory_space=pl.ANY),
         scratch_shapes=[pltpu.VMEM((n, 6, NLEV, NL), F32), pltpu.SemaphoreType.DMA((n,))],
         input_output_aliases={n: 0} if keep else {},
         cost_estimate=pl.CostEstimate(flops=1_000_000, bytes_accessed=220_000 * n, transcendentals=0),
         compiler_params=pltpu.CompilerParams(vmem_limit_bytes=24 << 20),
         name="place_rest" if keep else "place_first",
-    )(*[a for a, _ in blocks], *([out] if keep else []))
-
-
-def toward(block, d):
-    route = [(z * NC + c, (z ^ d) * NC + c) for z in range(NZ) for c in range(NC) if 0 <= z - c <= 6]
+    )(*rows, *([out] if keep else []))
+
+
+def toward(block, d, half):
+    route = [(z * NC + c, (z ^ d) * NC + (c ^ half)) for z in range(NZ) for c in range(NC) if d < 4 or 1 <= z <= 6]
     return lax.ppermute(block, ("zl", "core"), route)
 
 
-def swap_cores(blocks):
-    return lax.ppermute(jnp.stack(blocks), "core", [(0, 1), (1, 0)])
+SENDS = [(d, half) for d in (4, 5, 3, 6, 2, 7, 1, 0) for half in range(2)][:-2] + [(0, 1)]
 
 
 def on_device(fc_long, fc_short):
@@ -361,18 +357,15 @@
     r2 = lax.all_to_all(y, ("zl", "zh"), 0, 0, tiled=True)
     sre, sim, *far = far_pairs(r2.reshape(NZ, NH, SLOT, 128), merid_table())
     got = {}
-    for d in (4, 5, 6, 7):
-        got[d] = toward(far[d - 4], d)
     near = near_pairs(sre, sim)
-    got[0] = near[0]
-    for d in (3, 2, 1):
-        got[d] = toward(near[d], d)
-    early, late = (0, 1, 2, 3, 4, 5), (6, 7)
-    out = None
-    for group in (early, late):
-        swapped = swap_cores([got[d][1] for d in group])
-        blocks = [(got[d], 0) for d in group] + [(swapped, i) for i in range(len(group))]
-        out = place(group, blocks, out)
+    mine = [*near, *far]
+    for d, half in SENDS:
+        got[d, half] = toward(mine[2 * d + half], d, half)
+    got[0, 0] = near[0]
+    first = [(0, 0)] + SENDS[:6]
+    out = place(first, [got[b] for b in first])
+    rest = SENDS[6:]
+    out = place(rest, [got[b] for b in rest], out)
     out = out.reshape(2, NV, 1, KL, NLEV, NL)
     return jnp.swapaxes(out, 3, 4)
 

time: 179 us -> 172 us (0.961)
  the two profiles are of different devices: /device:TPU:97 before, /device:TPU:1 now
where the time goes in v5:
time: 172 us; the launch traced here: 171 us
  blocking collectives  94.3 us (55%)
  starting transfers between devices  48.1 us (28%)
  Pallas kernels  16.9 us (10%)
  waiting for transfers between devices  11.7 us (7%)
    all_to_all x1, blocking collectives, on_device(): r2 = lax.all_to_all(y, ('zl', 'zh'), 0, 0, tiled=True)  64.9 us
    ppermute x15, starting transfers between devices, toward(): return lax.ppermute(block, ('zl', 'core'), route)  48.1 us
    all_to_all x1, blocking collectives, on_device(): r = lax.all_to_all(z, ('core', 'x', 'y'), 0, 0, tiled=True)  29.4 us
    ppermute x15, waiting for transfers between devices, toward(): return lax.ppermute(block, ('zl', 'core'), route)  11.7 us
    pallas_call x1, Pallas kernels, zonal(): pl.pallas_call(zonal_kernel, out_shape=jax.ShapeDtypeStruct((32, LATP, 76...  6.08 us
    pallas_call x1, Pallas kernels, far_pairs(): pl.pallas_call(far_kernel, out_shape=[SPEC] * 2 + [ROWSET] * 8, in_specs=...  4.16 us
  transfers between devices with their start and end apart: 15, of which 3 were waited for; matrix products, arithmetic and copies ran while one was open for 0% of the time, Pallas kernels for 2%

profile of v5, /device:TPU:1, one launch (start us, length us, event | category | flops | bytes accessed | tf_op | source)
XLA Modules:
  0.0 171.3 jit_solution(2086654236349329422)
XLA Ops:
  0.0 6.1 %zonal.1 = bf16[32,24,768]{2,1,0:T(8,128)(2,1)} custom-call(bf16[66,8,1440]{2,1,0:T(8,128)(2,1)} %bitcast.19, bf16[66,8,1440]{2,1,0:T(8,128)(2,1)} %bitcast.20, f32[160,1024]{1,0:T(8,128)} %constant.4.clone.f_hbm), custom_call_target="tpu_custom_call" | custom-call | tf_op jit(solution)/shard_map/zonal/pallas_call | solution.py:136
  6.1 29.4 %all_to_all.10 = bf16[32,24,768]{2,1,0:T(8,128)(2,1)S(1)} all-to-all(bf16[32,24,768]{2,1,0:T(8,128)(2,1)} %zonal.1), channel_id=1, replica_groups=mesh['zl'=8,'core'=2,'x'=4,'zh'=2,'y'=4] {'core','x','y'}, dimensions={0} | all-to-all | bytes 2359296 | tf_op jit(solution)/shard_map/all_to_all | solution.py:355
  35.5 3.0 %split_waves.1 = bf16[16,264,128]{2,1,0:T(8,128)(2,1)S(1)} custom-call(bf16[2,16,24,768]{3,2,1,0:T(8,128)(2,1)S(1)} %bitcast.17), custom_call_target="tpu_custom_call" | custom-call | tf_op jit(solution)/shard_map/split_waves/pallas_call | solution.py:193
  38.5 0.0 copy-start
  38.5 64.9 %all_to_all.11 = bf16[16,264,128]{2,1,0:T(8,128)(2,1)S(1)} all-to-all(bf16[16,264,128]{2,1,0:T(8,128)(2,1)S(1)} %split_waves.1), channel_id=1, replica_groups=mesh['zl'=8,'core'=2,'x'=4,'zh'=2,'y'=4] {'zl','zh'}, dimensions={0} | all-to-all | bytes 2162688 | tf_op jit(solution)/shard_map/all_to_all | solution.py:357
  103.4 4.2 %far_pairs.1 = (f32[3,384,128]{2,1,0:T(8,128)S(1)}, f32[3,384,128]{2,1,0:T(8,128)S(1)}, bf16[96,384]{1,0:T(8,128)(2,1)S(1)}, bf16[96,384]{1,0:T(8,128)(2,1)S(1)}...) custom-call(bf16[8,2,264,128]{3,2,1,0:T(8,128)(2,1)S(1)} %bitcast.18, ...), custom_call_target="tpu_custom_call" | custom-call | tf_op jit(solution)/shard_map/far_pairs/pallas_call | solution.py:275
  107.6 1.3 collective-permute-start
  108.9 1.3 collective-permute-start.1
  110.2 0.7 collective-permute-start.4
  110.9 0.7 collective-permute-start.5
  111.6 1.3 collective-permute-start.9
  112.9 1.6 near_pairs.1
  114.4 4.0 %collective-permute-done.refs_0_ = bf16[96,384]{1,0:T(8,128)(2,1)S(1)} collective-permute-done((bf16[96,384]{1,0:T(8,128)(2,1)S(1)}, bf16[96,384]{1,0:T(8,128)(2,1)S(1)}, u32[]{:S(2)}, u32[]{:S(2)}) %collective-permute-start) | collective-permute-done | bytes 73760 | tf_op jit(solution)/shard_map/ppermute | solution.py:345
  118.4 1.3 collective-permute-start.10
  119.7 6.9 %collective-permute-done.1.refs_1_ = bf16[96,384]{1,0:T(8,128)(2,1)S(1)} collective-permute-done((bf16[96,384]{1,0:T(8,128)(2,1)S(1)}, bf16[96,384]{1,0:T(8,128)(2,1)S(1)}, u32[]{:S(2)}, u32[]{:S(2)}) %collective-permute-start.1) | collective-permute-done | bytes 73760 | tf_op jit(solution)/shard_map/ppermute | solution.py:345
  126.5 1.3 collective-permute-start.11
  127.8 0.0 collective-permute-done.4.refs_4_
  127.8 1.3 collective-permute-start.12
  129.2 22.5 %collective-permute-start.13 = (bf16[96,384]{1,0:T(8,128)(2,1)S(1)}, bf16[96,384]{1,0:T(8,128)(2,1)S(1)}, u32[]{:S(2)}, u32[]{:S(2)}) collective-permute-start(bf16[96,384]{1,0:T(8,128)(2,1)S(1)} %get-tuple-element.39), channel_id=1, source_target_pairs={{0,192},{32,224},{64,128},{96,160},{128,64},{160,96},{192,0},{224,... | collective-permute-start | bytes 221192 | tf_op jit(solution)/shard_map/ppermute | solution.py:345
  151.7 0.0 collective-permute-done.9.refs_1_
  151.7 2.2 %collective-permute-start.14 = (bf16[96,384]{1,0:T(8,128)(2,1)S(1)}, bf16[96,384]{1,0:T(8,128)(2,1)S(1)}, u32[]{:S(2)}, u32[]{:S(2)}) collective-permute-start(bf16[96,384]{1,0:T(8,128)(2,1)S(1)} %get-tuple-element.40), channel_id=1, source_target_pairs={{0,224},{32,192},{64,160},{96,128},{128,96},{160,64},{192,32},{224... | collective-permute-start | bytes 221192 | tf_op jit(solution)/shard_map/ppermute | solution.py:345
  153.9 1.9 %collective-permute-start.2 = (bf16[96,384]{1,0:T(8,128)(2,1)S(1)}, bf16[96,384]{1,0:T(8,128)(2,1)S(1)}, u32[]{:S(2)}, u32[]{:S(2)}) collective-permute-start(bf16[96,384]{1,0:T(8,128)(2,1)S(1)} %get-tuple-element.27), channel_id=1, source_target_pairs={{0,128},{32,160},{64,192},{96,224},{128,0},{160,32},{192,64},{224,... | collective-permute-start | bytes 221192 | tf_op jit(solution)/shard_map/ppermute | solution.py:345
  155.9 0.0 collective-permute-done.11.refs_3_
  155.9 4.8 %collective-permute-start.3 = (bf16[96,384]{1,0:T(8,128)(2,1)S(1)}, bf16[96,384]{1,0:T(8,128)(2,1)S(1)}, u32[]{:S(2)}, u32[]{:S(2)}) collective-permute-start(bf16[96,384]{1,0:T(8,128)(2,1)S(1)} %get-tuple-element.28), channel_id=1, source_target_pairs={{0,160},{32,128},{64,224},{96,192},{128,32},{160,0},{192,96},{224,... | collective-permute-start | bytes 221192 | tf_op jit(solution)/shard_map/ppermute | solution.py:345
  160.7 2.8 %collective-permute-start.6 = (bf16[96,384]{1,0:T(8,128)(2,1)S(1)}, bf16[96,384]{1,0:T(8,128)(2,1)S(1)}, u32[]{:S(2)}, u32[]{:S(2)}) collective-permute-start(bf16[96,384]{1,0:T(8,128)(2,1)S(1)} %get-tuple-element.31), channel_id=1, source_target_pairs={{0,64},{32,96},{64,0},{96,32},{128,192},{160,224},{192,128},{224,1... | collective-permute-start | bytes 221192 | tf_op jit(solution)/shard_map/ppermute | solution.py:345
  163.5 0.0 collective-permute-done.13.refs_5_
  163.5 2.5 %collective-permute-start.7 = (bf16[96,384]{1,0:T(8,128)(2,1)S(1)}, bf16[96,384]{1,0:T(8,128)(2,1)S(1)}, u32[]{:S(2)}, u32[]{:S(2)}) collective-permute-start(bf16[96,384]{1,0:T(8,128)(2,1)S(1)} %get-tuple-element.32), channel_id=1, source_target_pairs={{0,96},{32,64},{64,32},{96,0},{128,224},{160,192},{192,160},{224,1... | collective-permute-start | bytes 221192 | tf_op jit(solution)/shard_map/ppermute | solution.py:345
  166.0 0.0 collective-permute-done.14.refs_6_
  166.0 2.3 %collective-permute-start.8 = (bf16[96,384]{1,0:T(8,128)(2,1)S(1)}, bf16[96,384]{1,0:T(8,128)(2,1)S(1)}, u32[]{:S(2)}, u32[]{:S(2)}) collective-permute-start(bf16[96,384]{1,0:T(8,128)(2,1)S(1)} %get-tuple-element.33), channel_id=1, source_target_pairs={{0,32},{32,0},{64,96},{96,64},{128,160},{160,128},{192,224},{224,1... | collective-permute-start | bytes 221192 | tf_op jit(solution)/shard_map/ppermute | solution.py:345
  168.3 1.0 place_first.1.refs_9_
  169.4 0.8 collective-permute-done.7.refs_7_
  170.3 1.0 place_rest.1
  (8 shorter events, 0.0 us)
Async XLA Ops:
  38.5 64.9 %copy-start = (bf16[768,768]{1,0:T(8,128)(2,1)S(1)}, bf16[768,768]{1,0:T(8,128)(2,1)}, u32[]{:S(2)}) copy-start(bf16[768,768]{1,0:T(8,128)(2,1)} %constant.8.tab) | copy-start | bytes 3538948
  107.6 10.8 %collective-permute-start = (bf16[96,384]{1,0:T(8,128)(2,1)S(1)}, bf16[96,384]{1,0:T(8,128)(2,1)S(1)}, u32[]{:S(2)}, u32[]{:S(2)}) collective-permute-start(bf16[96,384]{1,0:T(8,128)(2,1)S(1)} %get-tuple-element.23), channel_id=1, source_target_pairs={{64,448},{96,480},{128,256},{160,288},{192,320},{224,352},{256,128... | collective-permute-start | bytes 221192 | tf_op jit(solution)/shard_map/ppermute | solution.py:345
  108.9 17.6 %collective-permute-start.1 = (bf16[96,384]{1,0:T(8,128)(2,1)S(1)}, bf16[96,384]{1,0:T(8,128)(2,1)S(1)}, u32[]{:S(2)}, u32[]{:S(2)}) collective-permute-start(bf16[96,384]{1,0:T(8,128)(2,1)S(1)} %get-tuple-element.24), channel_id=1, source_target_pairs={{64,480},{96,448},{128,288},{160,256},{192,352},{224,320},{256,160... | collective-permute-start | bytes 221192 | tf_op jit(solution)/shard_map/ppermute | solution.py:345
  110.2 17.6 %collective-permute-start.4 = (bf16[96,384]{1,0:T(8,128)(2,1)S(1)}, bf16[96,384]{1,0:T(8,128)(2,1)S(1)}, u32[]{:S(2)}, u32[]{:S(2)}) collective-permute-start(bf16[96,384]{1,0:T(8,128)(2,1)S(1)} %get-tuple-element.29), channel_id=1, source_target_pairs={{64,384},{96,416},{128,320},{160,352},{192,256},{224,288},{256,192... | collective-permute-start | bytes 221192 | tf_op jit(solution)/shard_map/ppermute | solution.py:345
  110.9 18.3 %collective-permute-start.5 = (bf16[96,384]{1,0:T(8,128)(2,1)S(1)}, bf16[96,384]{1,0:T(8,128)(2,1)S(1)}, u32[]{:S(2)}, u32[]{:S(2)}) collective-permute-start(bf16[96,384]{1,0:T(8,128)(2,1)S(1)} %get-tuple-element.30), channel_id=1, source_target_pairs={{64,416},{96,384},{128,352},{160,320},{192,288},{224,256},{256,224... | collective-permute-start | bytes 221192 | tf_op jit(solution)/shard_map/ppermute | solution.py:345
  111.6 40.2 %collective-permute-start.9 = (bf16[96,384]{1,0:T(8,128)(2,1)S(1)}, bf16[96,384]{1,0:T(8,128)(2,1)S(1)}, u32[]{:S(2)}, u32[]{:S(2)}) collective-permute-start(bf16[96,384]{1,0:T(8,128)(2,1)S(1)} %get-tuple-element.35), channel_id=1, source_target_pairs={{64,320},{96,352},{128,384},{160,416},{192,448},{224,480},{256,0},... | collective-permute-start | bytes 221192 | tf_op jit(solution)/shard_map/ppermute | solution.py:345
  118.4 35.5 %collective-permute-start.10 = (bf16[96,384]{1,0:T(8,128)(2,1)S(1)}, bf16[96,384]{1,0:T(8,128)(2,1)S(1)}, u32[]{:S(2)}, u32[]{:S(2)}) collective-permute-start(bf16[96,384]{1,0:T(8,128)(2,1)S(1)} %get-tuple-element.36), channel_id=1, source_target_pairs={{64,352},{96,320},{128,416},{160,384},{192,480},{224,448},{256,32}... | collective-permute-start | bytes 221192 | tf_op jit(solution)/shard_map/ppermute | solution.py:345
  126.5 29.3 %collective-permute-start.11 = (bf16[96,384]{1,0:T(8,128)(2,1)S(1)}, bf16[96,384]{1,0:T(8,128)(2,1)S(1)}, u32[]{:S(2)}, u32[]{:S(2)}) collective-permute-start(bf16[96,384]{1,0:T(8,128)(2,1)S(1)} %get-tuple-element.37), channel_id=1, source_target_pairs={{64,256},{96,288},{128,448},{160,480},{192,384},{224,416},{256,64}... | collective-permute-start | bytes 221192 | tf_op jit(solution)/shard_map/ppermute | solution.py:345
  127.8 32.9 %collective-permute-start.12 = (bf16[96,384]{1,0:T(8,128)(2,1)S(1)}, bf16[96,384]{1,0:T(8,128)(2,1)S(1)}, u32[]{:S(2)}, u32[]{:S(2)}) collective-permute-start(bf16[96,384]{1,0:T(8,128)(2,1)S(1)} %get-tuple-element.38), channel_id=1, source_target_pairs={{64,288},{96,256},{128,480},{160,448},{192,416},{224,384},{256,96}... | collective-permute-start | bytes 221192 | tf_op jit(solution)/shard_map/ppermute | solution.py:345
  129.2 34.4 %collective-permute-start.13 = (bf16[96,384]{1,0:T(8,128)(2,1)S(1)}, bf16[96,384]{1,0:T(8,128)(2,1)S(1)}, u32[]{:S(2)}, u32[]{:S(2)}) collective-permute-start(bf16[96,384]{1,0:T(8,128)(2,1)S(1)} %get-tuple-element.39), channel_id=1, source_target_pairs={{0,192},{32,224},{64,128},{96,160},{128,64},{160,96},{192,0},{224,... | collective-permute-start | bytes 221192 | tf_op jit(solution)/shard_map/ppermute | solution.py:345
  151.7 14.3 %collective-permute-start.14 = (bf16[96,384]{1,0:T(8,128)(2,1)S(1)}, bf16[96,384]{1,0:T(8,128)(2,1)S(1)}, u32[]{:S(2)}, u32[]{:S(2)}) collective-permute-start(bf16[96,384]{1,0:T(8,128)(2,1)S(1)} %get-tuple-element.40), channel_id=1, source_target_pairs={{0,224},{32,192},{64,160},{96,128},{128,96},{160,64},{192,32},{224... | collective-permute-start | bytes 221192 | tf_op jit(solution)/shard_map/ppermute | solution.py:345
  153.9 15.5 %collective-permute-start.2 = (bf16[96,384]{1,0:T(8,128)(2,1)S(1)}, bf16[96,384]{1,0:T(8,128)(2,1)S(1)}, u32[]{:S(2)}, u32[]{:S(2)}) collective-permute-start(bf16[96,384]{1,0:T(8,128)(2,1)S(1)} %get-tuple-element.27), channel_id=1, source_target_pairs={{0,128},{32,160},{64,192},{96,224},{128,0},{160,32},{192,64},{224,... | collective-permute-start | bytes 221192 | tf_op jit(solution)/shard_map/ppermute | solution.py:345
  155.9 13.5 %collective-permute-start.3 = (bf16[96,384]{1,0:T(8,128)(2,1)S(1)}, bf16[96,384]{1,0:T(8,128)(2,1)S(1)}, u32[]{:S(2)}, u32[]{:S(2)}) collective-permute-start(bf16[96,384]{1,0:T(8,128)(2,1)S(1)} %get-tuple-element.28), channel_id=1, source_target_pairs={{0,160},{32,128},{64,224},{96,192},{128,32},{160,0},{192,96},{224,... | collective-permute-start | bytes 221192 | tf_op jit(solution)/shard_map/ppermute | solution.py:345
  160.7 8.7 %collective-permute-start.6 = (bf16[96,384]{1,0:T(8,128)(2,1)S(1)}, bf16[96,384]{1,0:T(8,128)(2,1)S(1)}, u32[]{:S(2)}, u32[]{:S(2)}) collective-permute-start(bf16[96,384]{1,0:T(8,128)(2,1)S(1)} %get-tuple-element.31), channel_id=1, source_target_pairs={{0,64},{32,96},{64,0},{96,32},{128,192},{160,224},{192,128},{224,1... | collective-permute-start | bytes 221192 | tf_op jit(solution)/shard_map/ppermute | solution.py:345
  163.5 6.7 %collective-permute-start.7 = (bf16[96,384]{1,0:T(8,128)(2,1)S(1)}, bf16[96,384]{1,0:T(8,128)(2,1)S(1)}, u32[]{:S(2)}, u32[]{:S(2)}) collective-permute-start(bf16[96,384]{1,0:T(8,128)(2,1)S(1)} %get-tuple-element.32), channel_id=1, source_target_pairs={{0,96},{32,64},{64,32},{96,0},{128,224},{160,192},{192,160},{224,1... | collective-permute-start | bytes 221192 | tf_op jit(solution)/shard_map/ppermute | solution.py:345
  166.0 4.2 %collective-permute-start.8 = (bf16[96,384]{1,0:T(8,128)(2,1)S(1)}, bf16[96,384]{1,0:T(8,128)(2,1)S(1)}, u32[]{:S(2)}, u32[]{:S(2)}) collective-permute-start(bf16[96,384]{1,0:T(8,128)(2,1)S(1)} %get-tuple-element.33), channel_id=1, source_target_pairs={{0,32},{32,0},{64,96},{96,64},{128,160},{160,128},{192,224},{224,1... | collective-permute-start | bytes 221192 | tf_op jit(solution)/shard_map/ppermute | solution.py:345

commit v6 on v5

--- a/solution.py
+++ b/solution.py
@@ -210,8 +210,8 @@
         bre = [sre[jt, pl.ds(v * NS + s, NLEV, stride=VS), :] for s in range(NS)]
         bim = [sim[jt, pl.ds(v * NS + s, NLEV, stride=VS), :] for s in range(NS)]
         lanes = pl.ds(pl.multiple_of(jt * 128, 128), 128)
-        for i, out_ref in enumerate(outs):
-            base = ((zl ^ (first + i // 2)) * 2 + (core ^ (i % 2))) * VS + v * NS
+        for i, half in [(i, half) for i in range(len(outs)) for half in range(2)]:
+            base = ((zl ^ (first + i)) * 2 + (core ^ half)) * VS + v * NS
             co = jnp.zeros((NLEV, 128), F32)
             qd = jnp.zeros((NLEV, 128), F32)
             for s in range(NS):
@@ -219,15 +219,15 @@
                 ai = sim[jt, pl.ds(base + s, NLEV, stride=0), :]
                 co = co + ar * bre[s] + ai * bim[s]
                 qd = qd + ai * bre[s] - ar * bim[s]
-            out_ref[pl.ds(pl.multiple_of(v * 16, 16), 16), lanes] = (co * (1.0 / NS)).astype(BF16)
-            out_ref[pl.ds(pl.multiple_of(48 + v * 16, 16), 16), lanes] = (qd * (1.0 / NS)).astype(BF16)
+            outs[i][half, pl.ds(pl.multiple_of(v * 16, 16), 16), lanes] = (co * (1.0 / NS)).astype(BF16)
+            outs[i][half, pl.ds(pl.multiple_of(48 + v * 16, 16), 16), lanes] = (qd * (1.0 / NS)).astype(BF16)
         return carry
 
     lax.fori_loop(0, 3 * NV, block, 0)
 
 
 def far_kernel(r_ref, tab, sre, sim, *refs):
-    outs, a_ref = refs[:8], refs[8]
+    outs, a_ref = refs[:4], refs[4]
     tail = lax.broadcasted_iota(jnp.int32, (VS, 128), 1)
 
     def unpack(z, carry):
@@ -266,7 +266,7 @@
     products(sre, sim, outs, 0)
 
 
-ROWSET = jax.ShapeDtypeStruct((96, NL), BF16)
+ROWSET = jax.ShapeDtypeStruct((2, 96, NL), BF16)
 SPEC = jax.ShapeDtypeStruct((3, NLEV * VS, 128), F32)
 
 
@@ -274,9 +274,9 @@
     vm = pl.BlockSpec(memory_space=pltpu.VMEM)
     return pl.pallas_call(
         far_kernel,
-        out_shape=[SPEC] * 2 + [ROWSET] * 8,
+        out_shape=[SPEC] * 2 + [ROWSET] * 4,
         in_specs=[vm, vm],
-        out_specs=[vm] * 10,
+        out_specs=[vm] * 6,
         scratch_shapes=[pltpu.VMEM((NH, 768, 384), BF16)],
         compiler_params=pltpu.CompilerParams(vmem_limit_bytes=24 << 20),
         name="far_pairs",
@@ -287,9 +287,9 @@
     vm = pl.BlockSpec(memory_space=pltpu.VMEM)
     return pl.pallas_call(
         near_kernel,
-        out_shape=[ROWSET] * 8,
+        out_shape=[ROWSET] * 4,
         in_specs=[vm, vm],
-        out_specs=[vm] * 8,
+        out_specs=[vm] * 4,
         cost_estimate=pl.CostEstimate(flops=3_000_000_000, bytes_accessed=1_800_000, transcendentals=0),
         compiler_params=pltpu.CompilerParams(vmem_limit_bytes=16 << 20),
         name="near_pairs",
@@ -315,7 +315,7 @@
         @when_sent(blocks[i][0])
         def _():
             for cv in range(6):
-                bufs[i, cv] = rows[i][cv * 16 : (cv + 1) * 16, :].astype(F32)
+                bufs[i, cv] = rows[i][0, cv * 16 : (cv + 1) * 16, :].astype(F32)
             copy(i).start()
 
     for i in range(n):
@@ -327,25 +327,32 @@
 
 def place(blocks, rows, out=None):
     n, keep = len(blocks), int(out is not None)
+    specs = [pl.BlockSpec((1, 96, NL), lambda i, j=j: (j, 0, 0)) for _, j in rows]
     return pl.pallas_call(
         lambda *refs: place_kernel(blocks, keep, *refs),
         out_shape=jax.ShapeDtypeStruct((6, KL, NLEV, NL), F32),
-        in_specs=[pl.BlockSpec(memory_space=pltpu.VMEM)] * n + [pl.BlockSpec(memory_space=pl.ANY)] * keep,
+        grid=(1,),
+        in_specs=specs + [pl.BlockSpec(memory_space=pl.ANY)] * keep,
         out_specs=pl.BlockSpec(memory_space=pl.ANY),
         scratch_shapes=[pltpu.VMEM((n, 6, NLEV, NL), F32), pltpu.SemaphoreType.DMA((n,))],
         input_output_aliases={n: 0} if keep else {},
         cost_estimate=pl.CostEstimate(flops=1_000_000, bytes_accessed=220_000 * n, transcendentals=0),
         compiler_params=pltpu.CompilerParams(vmem_limit_bytes=24 << 20),
         name="place_rest" if keep else "place_first",
-    )(*rows, *([out] if keep else []))
-
-
-def toward(block, d, half):
-    route = [(z * NC + c, (z ^ d) * NC + (c ^ half)) for z in range(NZ) for c in range(NC) if d < 4 or 1 <= z <= 6]
+    )(*[a for a, _ in rows], *([out] if keep else []))
+
+
+def toward(block, d):
+    route = [(z * NC + c, (z ^ d) * NC + c) for z in range(NZ) for c in range(NC) if d < 4 or 1 <= z <= 6]
     return lax.ppermute(block, ("zl", "core"), route)
 
 
-SENDS = [(d, half) for d in (4, 5, 3, 6, 2, 7, 1, 0) for half in range(2)][:-2] + [(0, 1)]
+def swap_cores(blocks):
+    return lax.ppermute(jnp.stack(blocks), "core", [(0, 1), (1, 0)])
+
+
+SENDS = (4, 5, 6, 3, 7, 2, 1)
+GROUPS = ((0, 4, 5, 3), (6, 7, 2, 1))
 
 
 def on_device(fc_long, fc_short):
@@ -356,16 +363,16 @@
     y = split_waves(r.reshape(2, 16, LATP, 768))
     r2 = lax.all_to_all(y, ("zl", "zh"), 0, 0, tiled=True)
     sre, sim, *far = far_pairs(r2.reshape(NZ, NH, SLOT, 128), merid_table())
-    got = {}
+    out = None
     near = near_pairs(sre, sim)
     mine = [*near, *far]
-    for d, half in SENDS:
-        got[d, half] = toward(mine[2 * d + half], d, half)
-    got[0, 0] = near[0]
-    first = [(0, 0)] + SENDS[:6]
-    out = place(first, [got[b] for b in first])
-    rest = SENDS[6:]
-    out = place(rest, [got[b] for b in rest], out)
+    got = {0: near[0]}
+    for d in SENDS:
+        got[d] = toward(mine[d], d)
+    for group in GROUPS:
+        swapped = swap_cores([got[d][1] for d in group])
+        rows = [(got[d], 0) for d in group] + [(swapped, i) for i in range(len(group))]
+        out = place([(d, half) for half in range(2) for d in group], rows, out)
     out = out.reshape(2, NV, 1, KL, NLEV, NL)
     return jnp.swapaxes(out, 3, 4)
 

time: 172 us -> 160 us (0.930)
  waiting for transfers between devices: 11.7 us -> 2.01 us
  starting transfers between devices: 48.1 us -> 45.9 us
    ppermute x15 -> x7, starting transfers between devices: 48.1 us -> 24.9 us  [toward(): return lax.ppermute(block, ('zl', 'core'), route)]
    ppermute x0 -> x2, starting transfers between devices: none -> 21 us  [swap_cores(): return lax.ppermute(jnp.stack(blocks), 'core', [(0, 1), (1, 0)])]
    ppermute x15 -> x7, waiting for transfers between devices: 11.7 us -> 1.94 us  [toward(): return lax.ppermute(block, ('zl', 'core'), route)]
  transfers between devices with their start and end apart: 15 -> 9, of which waited for: 3 -> 2; matrix products, arithmetic and copies ran while one was open for 0% -> 0% of each run, Pallas kernels for 2% -> 2%
where the time goes in v6:
time: 160 us
  blocking collectives  94.3 us (59%)
  starting transfers between devices  45.9 us (29%)
  Pallas kernels  17 us (11%)
  waiting for transfers between devices  2.01 us (1%)
    all_to_all x1, blocking collectives, on_device(): r2 = lax.all_to_all(y, ('zl', 'zh'), 0, 0, tiled=True)  64.9 us
    all_to_all x1, blocking collectives, on_device(): r = lax.all_to_all(z, ('core', 'x', 'y'), 0, 0, tiled=True)  29.4 us
    ppermute x7, starting transfers between devices, toward(): return lax.ppermute(block, ('zl', 'core'), route)  24.9 us
    ppermute x2, starting transfers between devices, swap_cores(): return lax.ppermute(jnp.stack(blocks), 'core', [(0, 1), (1, 0)])  21 us
    pallas_call x1, Pallas kernels, zonal(): pl.pallas_call(zonal_kernel, out_shape=jax.ShapeDtypeStruct((32, LATP, 76...  6.08 us
    pallas_call x1, Pallas kernels, far_pairs(): pl.pallas_call(far_kernel, out_shape=[SPEC] * 2 + [ROWSET] * 4, in_specs=...  4.2 us
  transfers between devices with their start and end apart: 9, of which 2 were waited for; matrix products, arithmetic and copies ran while one was open for 0% of the time, Pallas kernels for 2%

profile of v6, /device:TPU:1, one launch (start us, length us, event | category | flops | bytes accessed | tf_op | source)
XLA Modules:
  0.0 159.7 jit_solution(6693850770661802393)
XLA Ops:
  0.0 6.1 %zonal.1 = bf16[32,24,768]{2,1,0:T(8,128)(2,1)} custom-call(bf16[66,8,1440]{2,1,0:T(8,128)(2,1)} %bitcast.19, bf16[66,8,1440]{2,1,0:T(8,128)(2,1)} %bitcast.20, f32[160,1024]{1,0:T(8,128)} %constant.4.clone.f_hbm), custom_call_target="tpu_custom_call" | custom-call | tf_op jit(solution)/shard_map/zonal/pallas_call | solution.py:136
  6.1 29.4 %all_to_all.10 = bf16[32,24,768]{2,1,0:T(8,128)(2,1)S(1)} all-to-all(bf16[32,24,768]{2,1,0:T(8,128)(2,1)} %zonal.1), channel_id=1, replica_groups=mesh['zl'=8,'core'=2,'x'=4,'zh'=2,'y'=4] {'core','x','y'}, dimensions={0} | all-to-all | bytes 2359296 | tf_op jit(solution)/shard_map/all_to_all | solution.py:362
  35.5 3.0 %split_waves.1 = bf16[16,264,128]{2,1,0:T(8,128)(2,1)S(1)} custom-call(bf16[2,16,24,768]{3,2,1,0:T(8,128)(2,1)S(1)} %bitcast.17), custom_call_target="tpu_custom_call" | custom-call | tf_op jit(solution)/shard_map/split_waves/pallas_call | solution.py:193
  38.5 0.0 copy-start
  38.5 64.9 %all_to_all.11 = bf16[16,264,128]{2,1,0:T(8,128)(2,1)S(1)} all-to-all(bf16[16,264,128]{2,1,0:T(8,128)(2,1)S(1)} %split_waves.1), channel_id=1, replica_groups=mesh['zl'=8,'core'=2,'x'=4,'zh'=2,'y'=4] {'zl','zh'}, dimensions={0} | all-to-all | bytes 2162688 | tf_op jit(solution)/shard_map/all_to_all | solution.py:364
  103.4 0.0 copy-done
  103.4 4.2 %far_pairs.1 = (f32[3,384,128]{2,1,0:T(8,128)S(1)}, f32[3,384,128]{2,1,0:T(8,128)S(1)}, bf16[2,96,384]{2,1,0:T(8,128)(2,1)S(1)}, bf16[2,96,384]{2,1,0:T(8,128)(2...) custom-call(bf16[8,2,264,128]{3,2,1,0:T(8,128)(2,1)S(1)} %bitcast.18, bf16[768,768]{1,0:T(8,128)(2,1)S(1)} %copy-done), custom_call_target="tpu_custom_call" | custom-call | tf_op jit(solution)/shard_map/far_pairs/pallas_call | solution.py:275
  107.6 1.3 collective-permute-start.5
  108.9 1.3 collective-permute-start.6
  110.2 1.6 %near_pairs.1 = (bf16[2,96,384]{2,1,0:T(8,128)(2,1)S(1)}, bf16[2,96,384]{2,1,0:T(8,128)(2,1)S(1)}, bf16[2,96,384]{2,1,0:T(8,128)(2,1)S(1)}, bf16[2,96,384]{2,1,0:T(8,128)(2,1)S(1)}) custom-call(f32[3,384,128]{2,1,0:T(8,128)S(1)} %get-tuple-element.17.sre, f32[3,384,128]{2,1,0:T(8,128)S(1)} %get-tuple-element.18.sim), custom_call_target="tpu_custom_call" | custom-call | flops 3000000000 | bytes 1800000 | tf_op jit(solution)/shard_map/near_pairs/pallas_call | solution.py:288
  111.9 9.0 %collective-permute-start.7 = (bf16[2,96,384]{2,1,0:T(8,128)(2,1)S(1)}, bf16[2,96,384]{2,1,0:T(8,128)(2,1)S(1)}, u32[]{:S(2)}, u32[]{:S(2)}) collective-permute-start(bf16[2,96,384]{2,1,0:T(8,128)(2,1)S(1)} %get-tuple-element.24), channel_id=1, source_target_pairs={{0,192},{32,224},{64,128},{96,160},{128,64},{160,96},{192,0},{224,... | collective-permute-start | bytes 442376 | tf_op jit(solution)/shard_map/ppermute | solution.py:347
  120.9 1.3 collective-permute-start
  122.2 0.7 collective-permute-start.1
  122.8 0.0 collective-permute-done.5.refs_1_
  122.8 8.5 %collective-permute-start.2 = (bf16[2,96,384]{2,1,0:T(8,128)(2,1)S(1)}, bf16[2,96,384]{2,1,0:T(8,128)(2,1)S(1)}, u32[]{:S(2)}, u32[]{:S(2)}) collective-permute-start(bf16[2,96,384]{2,1,0:T(8,128)(2,1)S(1)} %get-tuple-element.19), channel_id=1, source_target_pairs={{0,128},{32,160},{64,192},{96,224},{128,0},{160,32},{192,64},{224,... | collective-permute-start | bytes 442376 | tf_op jit(solution)/shard_map/ppermute | solution.py:347
  131.4 1.9 %collective-permute-done.6.refs_2_ = bf16[2,96,384]{2,1,0:T(8,128)(2,1)S(1)} collective-permute-done((bf16[2,96,384]{2,1,0:T(8,128)(2,1)S(1)}, bf16[2,96,384]{2,1,0:T(8,128)(2,1)S(1)}, u32[]{:S(2)}, u32[]{:S(2)}) %collective-permute-start.6) | collective-permute-done | bytes 147488 | tf_op jit(solution)/shard_map/ppermute | solution.py:347
  133.3 2.8 %collective-permute-start.3 = (bf16[2,96,384]{2,1,0:T(8,128)(2,1)S(1)}, bf16[2,96,384]{2,1,0:T(8,128)(2,1)S(1)}, u32[]{:S(2)}, u32[]{:S(2)}) collective-permute-start(bf16[2,96,384]{2,1,0:T(8,128)(2,1)S(1)} %get-tuple-element.20), channel_id=1, source_target_pairs={{0,64},{32,96},{64,0},{96,32},{128,192},{160,224},{192,128},{224,1... | collective-permute-start | bytes 442376 | tf_op jit(solution)/shard_map/ppermute | solution.py:347
  136.2 0.0 collective-permute-done.7.refs_3_
  136.2 0.1 pad_maximum_fusion.1
  136.3 18.2 %collective-permute-start.8 = (bf16[4,96,384]{2,1,0:T(8,128)(2,1)S(1)}, bf16[4,96,384]{2,1,0:T(8,128)(2,1)S(1)}, u32[]{:S(2)}, u32[]{:S(2)}) collective-permute-start(bf16[4,96,384]{2,1,0:T(8,128)(2,1)S(1)} %pad_maximum_fusion.1), channel_id=1, source_target_pairs={{0,32},{32,0},{1,33},{33,1},{2,34},{34,2},{3,35},{35,3},{4,36},{36... | collective-permute-start | bytes 884744 | tf_op jit(solution)/shard_map/ppermute | solution.py:351
  154.5 0.0 collective-permute-done.refs_0_
  154.5 0.0 collective-permute-done.1.refs_1_
  154.5 0.0 collective-permute-done.2.refs_2_
  154.5 0.0 collective-permute-done.3.refs_3_
  154.6 0.1 pad_maximum_fusion
  154.6 2.9 %collective-permute-start.4 = (bf16[4,96,384]{2,1,0:T(8,128)(2,1)S(1)}, bf16[4,96,384]{2,1,0:T(8,128)(2,1)S(1)}, u32[]{:S(2)}, u32[]{:S(2)}) collective-permute-start(bf16[4,96,384]{2,1,0:T(8,128)(2,1)S(1)} %pad_maximum_fusion), channel_id=1, source_target_pairs={{0,32},{32,0},{1,33},{33,1},{2,34},{34,2},{3,35},{35,3},{4,36},{36... | collective-permute-start | bytes 884744 | tf_op jit(solution)/shard_map/ppermute | solution.py:351
  157.5 0.0 collective-permute-done.8.refs_4_.refs_5_.refs_6_.refs_7_
  157.5 1.1 place_first.1.refs_8_
  158.6 0.1 collective-permute-done.4.refs_4_.refs_5_.refs_6_.refs_7_
  158.7 1.0 place_rest.1
  (8 shorter events, 0.1 us)
Async XLA Ops:
  38.5 64.9 %copy-start = (bf16[768,768]{1,0:T(8,128)(2,1)S(1)}, bf16[768,768]{1,0:T(8,128)(2,1)}, u32[]{:S(2)}) copy-start(bf16[768,768]{1,0:T(8,128)(2,1)} %constant.8.tab) | copy-start | bytes 3538948
  107.6 15.2 %collective-permute-start.5 = (bf16[2,96,384]{2,1,0:T(8,128)(2,1)S(1)}, bf16[2,96,384]{2,1,0:T(8,128)(2,1)S(1)}, u32[]{:S(2)}, u32[]{:S(2)}) collective-permute-start(bf16[2,96,384]{2,1,0:T(8,128)(2,1)S(1)} %get-tuple-element.22), channel_id=1, source_target_pairs={{64,320},{96,352},{128,384},{160,416},{192,448},{224,480},{256,0},... | collective-permute-start | bytes 442376 | tf_op jit(solution)/shard_map/ppermute | solution.py:347
  108.9 24.4 %collective-permute-start.6 = (bf16[2,96,384]{2,1,0:T(8,128)(2,1)S(1)}, bf16[2,96,384]{2,1,0:T(8,128)(2,1)S(1)}, u32[]{:S(2)}, u32[]{:S(2)}) collective-permute-start(bf16[2,96,384]{2,1,0:T(8,128)(2,1)S(1)} %get-tuple-element.23), channel_id=1, source_target_pairs={{64,256},{96,288},{128,448},{160,480},{192,384},{224,416},{256,64}... | collective-permute-start | bytes 442376 | tf_op jit(solution)/shard_map/ppermute | solution.py:347
  111.9 24.3 %collective-permute-start.7 = (bf16[2,96,384]{2,1,0:T(8,128)(2,1)S(1)}, bf16[2,96,384]{2,1,0:T(8,128)(2,1)S(1)}, u32[]{:S(2)}, u32[]{:S(2)}) collective-permute-start(bf16[2,96,384]{2,1,0:T(8,128)(2,1)S(1)} %get-tuple-element.24), channel_id=1, source_target_pairs={{0,192},{32,224},{64,128},{96,160},{128,64},{160,96},{192,0},{224,... | collective-permute-start | bytes 442376 | tf_op jit(solution)/shard_map/ppermute | solution.py:347
  120.9 33.6 %collective-permute-start = (bf16[2,96,384]{2,1,0:T(8,128)(2,1)S(1)}, bf16[2,96,384]{2,1,0:T(8,128)(2,1)S(1)}, u32[]{:S(2)}, u32[]{:S(2)}) collective-permute-start(bf16[2,96,384]{2,1,0:T(8,128)(2,1)S(1)} %get-tuple-element.15), channel_id=1, source_target_pairs={{64,448},{96,480},{128,256},{160,288},{192,320},{224,352},{256,128... | collective-permute-start | bytes 442376 | tf_op jit(solution)/shard_map/ppermute | solution.py:347
  122.2 32.3 %collective-permute-start.1 = (bf16[2,96,384]{2,1,0:T(8,128)(2,1)S(1)}, bf16[2,96,384]{2,1,0:T(8,128)(2,1)S(1)}, u32[]{:S(2)}, u32[]{:S(2)}) collective-permute-start(bf16[2,96,384]{2,1,0:T(8,128)(2,1)S(1)} %get-tuple-element.16), channel_id=1, source_target_pairs={{64,384},{96,416},{128,320},{160,352},{192,256},{224,288},{256,192... | collective-permute-start | bytes 442376 | tf_op jit(solution)/shard_map/ppermute | solution.py:347
  122.8 31.7 %collective-permute-start.2 = (bf16[2,96,384]{2,1,0:T(8,128)(2,1)S(1)}, bf16[2,96,384]{2,1,0:T(8,128)(2,1)S(1)}, u32[]{:S(2)}, u32[]{:S(2)}) collective-permute-start(bf16[2,96,384]{2,1,0:T(8,128)(2,1)S(1)} %get-tuple-element.19), channel_id=1, source_target_pairs={{0,128},{32,160},{64,192},{96,224},{128,0},{160,32},{192,64},{224,... | collective-permute-start | bytes 442376 | tf_op jit(solution)/shard_map/ppermute | solution.py:347
  133.3 21.2 %collective-permute-start.3 = (bf16[2,96,384]{2,1,0:T(8,128)(2,1)S(1)}, bf16[2,96,384]{2,1,0:T(8,128)(2,1)S(1)}, u32[]{:S(2)}, u32[]{:S(2)}) collective-permute-start(bf16[2,96,384]{2,1,0:T(8,128)(2,1)S(1)} %get-tuple-element.20), channel_id=1, source_target_pairs={{0,64},{32,96},{64,0},{96,32},{128,192},{160,224},{192,128},{224,1... | collective-permute-start | bytes 442376 | tf_op jit(solution)/shard_map/ppermute | solution.py:347
  136.3 21.2 %collective-permute-start.8 = (bf16[4,96,384]{2,1,0:T(8,128)(2,1)S(1)}, bf16[4,96,384]{2,1,0:T(8,128)(2,1)S(1)}, u32[]{:S(2)}, u32[]{:S(2)}) collective-permute-start(bf16[4,96,384]{2,1,0:T(8,128)(2,1)S(1)} %pad_maximum_fusion.1), channel_id=1, source_target_pairs={{0,32},{32,0},{1,33},{33,1},{2,34},{34,2},{3,35},{35,3},{4,36},{36... | collective-permute-start | bytes 884744 | tf_op jit(solution)/shard_map/ppermute | solution.py:351
  154.6 4.1 %collective-permute-start.4 = (bf16[4,96,384]{2,1,0:T(8,128)(2,1)S(1)}, bf16[4,96,384]{2,1,0:T(8,128)(2,1)S(1)}, u32[]{:S(2)}, u32[]{:S(2)}) collective-permute-start(bf16[4,96,384]{2,1,0:T(8,128)(2,1)S(1)} %pad_maximum_fusion), channel_id=1, source_target_pairs={{0,32},{32,0},{1,33},{33,1},{2,34},{34,2},{3,35},{35,3},{4,36},{36... | collective-permute-start | bytes 884744 | tf_op jit(solution)/shard_map/ppermute | solution.py:351
